TPU v7x, 32 devices: a whole 2x2x4 slice. The times are simulated.
32 devices in a mesh: edata: 4 (over z), expert: 8 (over y, x, core).
Axes of the slice: x: 2, y: 2, z: 4, core: 2. Of those that a mesh axis runs over, the one named last changes fastest.
Arguments:
- tokens: bfloat16 [1024, 4096], P('expert', 'edata'), may hold values from -6 to 6
- grad_out: bfloat16 [1024, 4096], P('expert', 'edata'), may hold values from -6 to 6
- expert_ids: int32 [1024, 8], P('expert'), may hold values from 0 to 15, all different within a row; in each aligned block of 128 rows (0 to 127, 128 to 255, ...) at most 80 rows name the same one
- route_prob: float32 [1024, 8], P('expert'), may hold values from 0.05 to 0.5
- w_gate: bfloat16 [16, 1024, 4096], P('expert', 'edata'), may hold values from -0.09375 to 0.09375
- w_up: bfloat16 [16, 1024, 4096], P('expert', 'edata'), may hold values from -0.09375 to 0.09375
- w_down: bfloat16 [16, 1024, 4096], P('expert', 'edata'), may hold values from -0.1875 to 0.1875
Outputs:
- grad_tokens: bfloat16 [1024, 4096], P('expert', 'edata')
- grad_gate: bfloat16 [16, 1024, 4096], P('expert', 'edata')
- grad_up: bfloat16 [16, 1024, 4096], P('expert', 'edata')
- grad_down: bfloat16 [16, 1024, 4096], P('expert', 'edata')
Inputs may be any that keep to these rules, and one draw needn't show every extreme that they name: `expert_ids`: each token names 8 different experts. Among the tokens of one aligned block of 128 no expert is named more than 80 times, and in every draw some expert is named exactly 80 times in some block.
All inputs are finite; a program needn't handle non-finite values.
Results may differ from a plain program's by a relative error of at most 0.012.
Values may be sent and summed in bfloat16 or wider, within the bound.
A program may use at most 192 MiB of HBM per device.

v0:
```python
import jax
import jax.numpy as jnp
from jax import lax
from jax.sharding import PartitionSpec as P


def body(tokens, grad_out, expert_ids, route_prob, w_gate, w_up, w_down):
    token_count, top_count = expert_ids.shape
    local_experts = w_gate.shape[0]
    expert_devices = lax.axis_size("expert")
    experts_all = expert_devices * local_experts
    capacity = token_count * top_count * 5 // (4 * experts_all)
    pair_count = token_count * top_count
    flat_ids = expert_ids.reshape(pair_count)
    onehot = (flat_ids[:, None] == jnp.arange(experts_all, dtype=jnp.int32)[None, :]).astype(
        jnp.int32
    )
    earlier = jnp.cumsum(onehot, 0) - onehot
    slots = jnp.sum(earlier * onehot, 1)
    target = flat_ids * capacity + slots
    sender = jnp.full((experts_all * capacity,), pair_count, jnp.int32)
    sender = sender.at[target].set(jnp.arange(pair_count, dtype=jnp.int32))
    token_of = sender // top_count
    whole_x, whole_dy = (
        lax.all_gather(tokens, "edata", axis=1, tiled=True),
        lax.all_gather(grad_out, "edata", axis=1, tiled=True),
    )
    width = whole_x.shape[1]
    padded_x = jnp.concatenate([whole_x, jnp.zeros((1, width), jnp.bfloat16)], 0)
    scaled = (
        (route_prob[:, :, None] * whole_dy[:, None, :])
        .astype(jnp.bfloat16)
        .reshape(pair_count, width)
    )
    padded_s = jnp.concatenate([scaled, jnp.zeros((1, width), jnp.bfloat16)], 0)
    sent_x = padded_x[token_of].reshape(expert_devices, local_experts * capacity, width)
    sent_dy = padded_s[sender].reshape(expert_devices, local_experts * capacity, width)
    sent_x, sent_dy = (sent_x, sent_dy)
    recv_x, recv_dy = (
        lax.all_to_all(sent_x, "expert", split_axis=0, concat_axis=0, tiled=True),
        lax.all_to_all(sent_dy, "expert", split_axis=0, concat_axis=0, tiled=True),
    )
    slot_x = recv_x.reshape(expert_devices, local_experts, capacity, -1)
    slot_dy = recv_dy.reshape(expert_devices, local_experts, capacity, -1)
    gate_value = jnp.einsum("sxcd,xfd->sxcf", slot_x, w_gate, preferred_element_type=jnp.float32)
    up_value = jnp.einsum("sxcd,xfd->sxcf", slot_x, w_up, preferred_element_type=jnp.float32)
    sigma = jax.nn.sigmoid(gate_value)
    active = gate_value * sigma
    hidden = (active * up_value).astype(jnp.bfloat16)
    back = jnp.einsum("sxcd,xfd->sxcf", slot_dy, w_down, preferred_element_type=jnp.float32)
    gate_grad = (back * up_value * sigma * (1.0 + gate_value * (1.0 - sigma))).astype(jnp.bfloat16)
    up_grad = (back * active).astype(jnp.bfloat16)
    grad_gate = jnp.einsum(
        "sxcf,sxcd->xfd", gate_grad, slot_x, preferred_element_type=jnp.float32
    ).astype(jnp.bfloat16)
    grad_up = jnp.einsum(
        "sxcf,sxcd->xfd", up_grad, slot_x, preferred_element_type=jnp.float32
    ).astype(jnp.bfloat16)
    grad_down = jnp.einsum(
        "sxcf,sxcd->xfd", hidden, slot_dy, preferred_element_type=jnp.float32
    ).astype(jnp.bfloat16)
    partial_value = jnp.einsum(
        "sxcf,xfd->sxcd", gate_grad, w_gate, preferred_element_type=jnp.float32
    )
    partial_value = partial_value + jnp.einsum(
        "sxcf,xfd->sxcd", up_grad, w_up, preferred_element_type=jnp.float32
    )
    partial_value = partial_value.astype(jnp.bfloat16)
    returned = lax.all_to_all(
        partial_value.reshape(expert_devices, local_experts * capacity, -1),
        "expert",
        split_axis=0,
        concat_axis=0,
        tiled=True,
    )
    width = returned.shape[-1]
    picked = returned.reshape(experts_all * capacity, width)[target]
    per_token = jnp.sum(picked.reshape(token_count, top_count, width), 1, dtype=jnp.float32)
    grad_tokens = lax.psum_scatter(per_token, "edata", scatter_dimension=1, tiled=True).astype(
        jnp.bfloat16
    )
    return (grad_tokens, grad_gate, grad_up, grad_down)


def solution(mesh):
    placed = (
        P("expert", "edata"),
        P("expert", "edata"),
        P("expert", None),
        P("expert", None),
        P("expert", "edata", None),
        P("expert", "edata", None),
        P("expert", "edata", None),
    )
    return jax.shard_map(
        body,
        mesh=mesh,
        in_specs=placed,
        out_specs=(
            P("expert", "edata"),
            P("expert", "edata", None),
            P("expert", "edata", None),
            P("expert", "edata", None),
        ),
        check_vma=False,
    )
```

profile of v0, /device:TPU:0, one launch (start us, length us, event | category | flops | bytes accessed | tf_op | source)
XLA Modules:
  0.0 546.0 jit_solution(8760794174096931553)
XLA Ops:
  7.2 0.0 all-gather.5.cloned.1.call-start
  7.2 0.7 all-gather.5.cloned.1.call-update
  7.9 0.8 copy.15
  8.7 0.1 eq.29
  8.8 0.1 eq.25
  8.9 0.7 broadcast_multiply_fusion
  9.6 0.1 copy.14
  9.7 0.1 mul.65
  9.8 4.5 reduce-window.6
  14.3 0.1 slice.14
  14.4 0.1 copy.17
  14.5 0.1 copy.18
  14.6 0.1 broadcast_add_fusion
  14.8 4.3 scatter_custom_fusion
  19.1 21.1 %all-gather.5.cloned.1.call-done = bf16[128,4096]{1,0:T(8,128)(2,1)} async-done(((bf16[128,1024]{1,0:T(8,128)(2,1)}), bf16[128,4096]{1,0:T(8,128)(2,1)}) %all-gather.5.cloned.1.call-update) | async-done | bytes 1048592 | tf_op jit(solution)/shard_map/all_gather | solution.py:25
  40.3 1.3 concatenate.7
  41.6 8.3 %gather_fusion.1 = bf16[1280,4096]{1,0:T(8,128)(2,1)} fusion(bf16[129,4096]{1,0:T(8,128)(2,1)S(1)} %concatenate.7, s32[2048]{0:T(1024)S(1)} %pad_clamp_fusion), kind=kCustom, calls=%fused_computation.1 | custom fusion | bytes 20976640 | tf_op jit(solution)/shard_map/gather | solution.py:36
  49.9 5.3 all-to-all-start.1
  55.2 0.0 all-gather.3.cloned.1.call-start
  55.3 0.7 all-gather.3.cloned.1.call-update
  56.0 0.1 copy.13
  56.1 0.1 mul.58
  56.2 29.2 %all-gather.3.cloned.1.call-done = bf16[128,4096]{1,0:T(8,128)(2,1)} async-done(((bf16[128,1024]{1,0:T(8,128)(2,1)}), bf16[128,4096]{1,0:T(8,128)(2,1)}) %all-gather.3.cloned.1.call-update) | async-done | bytes 1048592 | tf_op jit(solution)/shard_map/all_gather | solution.py:26
  85.4 1.4 convert_element_type.48
  86.8 5.5 %fusion = bf16[1024,4096]{1,0:T(8,128)(2,1)} fusion(f32[128,4096]{1,0:T(8,128)S(1)} %convert_element_type.48, f32[1024]{0:T(1024)S(1)} %mul.58), kind=kLoop, calls=%fused_computation.7 | loop fusion | flops 8388608 | bytes 10489856 | tf_op jit(solution)/shard_map/convert_element_type | solution.py:32
  92.3 7.8 %concatenate.6 = bf16[1025,4096]{1,0:T(8,128)(2,1)} pad(bf16[1024,4096]{1,0:T(8,128)(2,1)} %fusion, bf16[]{:T(256)} %constant.11.clone.1), padding=0_1x0_0 | pad | bytes 16785410 | tf_op jit(solution)/shard_map/concatenate | solution.py:35
  100.1 23.2 %gather_fusion = bf16[1280,4096]{1,0:T(8,128)(2,1)} fusion(bf16[1025,4096]{1,0:T(8,128)(2,1)} %concatenate.6, s32[2048]{0:T(1024)S(1)} %pad_clamp_fusion.1), kind=kCustom, calls=%fused_computation | custom fusion | bytes 20976640 | tf_op jit(solution)/shard_map/gather | solution.py:37
  123.2 48.5 %all-to-all-done.1 = bf16[8,160,4096]{2,1,0:T(8,128)(2,1)} async-done(((bf16[8,160,4096]{2,1,0:T(8,128)(2,1)}), bf16[8,160,4096]{2,1,0:T(8,128)(2,1)}, u32[]{:S(2)}, u32[]{:S(2)}) %all-to-all-start.1) | async-done | bytes 10485792 | tf_op jit(solution)/shard_map/all_to_all | solution.py:40
  171.7 5.4 all-to-all-start
  177.1 0.0 copy-start.1
  177.1 9.3 %fusion.31 = f32[8,2,80,256]{3,2,0,1:T(8,128)} fusion(bf16[2,256,4096]{2,1,0:T(8,128)(2,1)} %param.11, bf16[8,2,80,4096]{3,2,1,0:T(8,128)(2,1)} %bitcast.11), kind=kOutput, calls=%fused_computation.31 | convolution fusion | flops 2684354560 | bytes 15990784 | tf_op jit(solution)/shard_map/sxcd,xfd->sxcf/dot_general | solution.py:45
  186.4 8.3 %fusion.26 = f32[8,2,80,256]{3,2,0,1:T(8,128)} fusion(bf16[2,256,4096]{2,1,0:T(8,128)(2,1)S(1)} %copy-done.1, bf16[8,2,80,4096]{3,2,1,0:T(8,128)(2,1)} %bitcast.11), kind=kOutput, calls=%fused_computation.30 | convolution fusion | flops 2684354560 | bytes 15990784 | tf_op jit(solution)/shard_map/sxcd,xfd->sxcf/dot_general | solution.py:46
  194.7 98.9 %all-to-all-done = bf16[8,160,4096]{2,1,0:T(8,128)(2,1)} async-done(((bf16[8,160,4096]{2,1,0:T(8,128)(2,1)}), bf16[8,160,4096]{2,1,0:T(8,128)(2,1)}, u32[]{:S(2)}, u32[]{:S(2)}) %all-to-all-start) | async-done | bytes 10485792 | tf_op jit(solution)/shard_map/all_to_all | solution.py:41
  293.7 9.4 %multiply_convert_fusion.1 = (bf16[8,2,80,256]{3,2,0,1:T(8,128)(2,1)S(1)}, bf16[8,2,80,256]{3,2,0,1:T(8,128)(2,1)S(1)}) fusion(f32[8,2,80,256]{3,2,0,1:T(8,128)} %fusion.31, f32[8,2,80,256]{3,2,0,1:T(8,128)} %fusion.26, bf16[2,256,4096]{2,1,0:T(8,128)(2,1)} %param.13, bf16[8,2,80,4096]{3,2,1,0:T(8,128)(2,1)} %bitcast.6), kind=kOutput, calls=%fused_computation.34 | convolution fusion | flops 2688614400 | bytes 18612224 | tf_op jit(solution)/shard_map/sxcd,xfd->sxcf/dot_general | solution.py:50
  303.0 8.5 %fusion.20 = f32[2,8,80,4096]{3,2,1,0:T(8,128)} fusion(bf16[8,2,80,256]{3,2,0,1:T(8,128)(2,1)S(1)} %get-tuple-element.5, bf16[2,256,4096]{2,1,0:T(8,128)(2,1)S(1)} %copy-done), kind=kOutput, calls=%fused_computation.24 | convolution fusion | flops 2684354560 | bytes 25821184 | tf_op jit(solution)/shard_map/sxcf,xfd->sxcd/dot_general | solution.py:62
  311.6 22.6 %fusion.1 = bf16[8,2,80,4096]{3,2,0,1:T(8,128)(2,1)} fusion(f32[2,8,80,4096]{3,2,1,0:T(8,128)} %fusion.20, bf16[8,2,80,256]{3,2,0,1:T(8,128)(2,1)S(1)} %get-tuple-element.4, bf16[2,256,4096]{2,1,0:T(8,128)(2,1)} %param.12), kind=kOutput, calls=%fused_computation.8 | convolution fusion | flops 2694840320 | bytes 36306944 | tf_op jit(solution)/shard_map/sxcf,xfd->sxcd/dot_general | solution.py:65
  334.2 9.4 %copy.22 = bf16[8,2,80,4096]{3,2,1,0:T(8,128)(2,1)} copy(bf16[8,2,80,4096]{3,2,0,1:T(8,128)(2,1)} %fusion.1) | data formatting | bytes 20971520 | tf_op jit(solution)/shard_map/convert_element_type | solution.py:68
  343.6 5.1 all-to-all-start.2
  348.8 0.0 reduce-scatter.2.cloned.1.call-start
  348.8 116.4 %all-to-all-done.2 = bf16[8,160,4096]{2,1,0:T(8,128)(2,1)} async-done(((bf16[8,160,4096]{2,1,0:T(8,128)(2,1)}), bf16[8,160,4096]{2,1,0:T(8,128)(2,1)}, u32[]{:S(2)}, u32[]{:S(2)}) %all-to-all-start.2) | async-done | bytes 10485792 | tf_op jit(solution)/shard_map/all_to_all | solution.py:69
  465.3 20.4 %gather_fusion.2 = bf16[1024,4096]{1,0:T(8,128)(2,1)} fusion(bf16[1280,4096]{1,0:T(8,128)(2,1)} %bitcast.21, s32[1024]{0:T(1024)S(1)} %broadcast_clamp_fusion), kind=kCustom, calls=%fused_computation.2 | custom fusion | bytes 16781312 | tf_op jit(solution)/shard_map/gather | solution.py:77
  485.7 10.3 %convert_reduce_fusion = f32[128,4096]{1,0:T(8,128)} fusion(bf16[1024,4096]{1,0:T(8,128)(2,1)} %gather_fusion.2), kind=kLoop, calls=%fused_computation.5 | loop fusion | flops 7864320 | bytes 10485760 | tf_op jit(solution)/shard_map/reduce_sum | solution.py:78
  496.1 0.0 reduce-scatter.2.cloned.1.call-update
  496.1 9.2 %bitcast_convert_fusion.1 = bf16[2,256,4096]{2,1,0:T(8,128)(2,1)} fusion(bf16[8,2,80,256]{3,2,0,1:T(8,128)(2,1)S(1)} %get-tuple-element.4, bf16[8,2,80,4096]{3,2,1,0:T(8,128)(2,1)} %bitcast.11), kind=kOutput, calls=%fused_computation.14 | convolution fusion | flops 2686451712 | bytes 15335424 | tf_op jit(solution)/shard_map/sxcf,sxcd->xfd/dot_general | solution.py:56
  505.3 9.4 %bitcast_convert_fusion.2 = bf16[2,256,4096]{2,1,0:T(8,128)(2,1)} fusion(bf16[8,2,80,256]{3,2,0,1:T(8,128)(2,1)S(1)} %get-tuple-element.5, bf16[8,2,80,4096]{3,2,1,0:T(8,128)(2,1)} %bitcast.11), kind=kOutput, calls=%fused_computation.15 | convolution fusion | flops 2686451712 | bytes 15335424 | tf_op jit(solution)/shard_map/sxcf,sxcd->xfd/dot_general | solution.py:53
  514.8 9.7 %bitcast_convert_fusion = bf16[2,256,4096]{2,1,0:T(8,128)(2,1)} fusion(bf16[8,2,80,4096]{3,2,1,0:T(8,128)(2,1)} %bitcast.6, f32[8,2,80,256]{3,2,0,1:T(8,128)S(1)} %copy-done.4, f32[8,2,80,256]{3,2,0,1:T(8,128)S(1)} %copy-done.3), kind=kOutput, calls=%fused_computation.13 | convolution fusion | flops 2688417792 | bytes 17301504 | tf_op jit(solution)/shard_map/sxcf,sxcd->xfd/dot_general | solution.py:59
  524.5 12.9 %reduce-scatter.2.cloned.1.call-done = f32[128,1024]{1,0:T(8,128)} async-done(((f32[128,4096]{1,0:T(8,128)}), f32[128,1024]{1,0:T(8,128)}) %reduce-scatter.2.cloned.1.call-update) | async-done | bytes 524304 | tf_op jit(solution)/shard_map/reduce_scatter | solution.py:79
  537.5 1.8 convert_element_type.58
  (19 shorter events, 0.1 us)
Async XLA Ops:
  7.2 33.1 %all-gather.5.cloned.1.call-start = ((), (), s32[]{:S(2)}) async-start(), calls=%async_computation.5 | async-start | bytes 1310720 | tf_op jit(solution)/shard_map/all_gather | solution.py:25
  49.9 6.0 %copy-start.2 = (f32[128,8]{0,1:T(8,128)S(1)}, f32[128,8]{0,1:T(8,128)}, u32[]{:S(2)}) copy-start(f32[128,8]{0,1:T(8,128)} %param.10) | copy-start | bytes 12292
  49.9 121.8 %all-to-all-start.1 = ((bf16[8,160,4096]{2,1,0:T(8,128)(2,1)}), bf16[8,160,4096]{2,1,0:T(8,128)(2,1)}, u32[]{:S(2)}, u32[]{:S(2)}) async-start(bf16[8,160,4096]{2,1,0:T(8,128)(2,1)} %bitcast.82), calls=%async_computation.1 | async-start | bytes 20971520 | tf_op jit(solution)/shard_map/all_to_all | solution.py:40
  55.2 30.2 %all-gather.3.cloned.1.call-start = ((), (), s32[]{:S(2)}) async-start(), calls=%async_computation.4 | async-start | bytes 1310720 | tf_op jit(solution)/shard_map/all_gather | solution.py:26
  171.7 121.9 %all-to-all-start = ((bf16[8,160,4096]{2,1,0:T(8,128)(2,1)}), bf16[8,160,4096]{2,1,0:T(8,128)(2,1)}, u32[]{:S(2)}, u32[]{:S(2)}) async-start(bf16[8,160,4096]{2,1,0:T(8,128)(2,1)} %bitcast.83), calls=%async_computation | async-start | bytes 20971520 | tf_op jit(solution)/shard_map/all_to_all | solution.py:41
  177.1 9.3 %copy-start.1 = (bf16[2,256,4096]{2,1,0:T(8,128)(2,1)S(1)}, bf16[2,256,4096]{2,1,0:T(8,128)(2,1)}, u32[]{:S(2)}) copy-start(bf16[2,256,4096]{2,1,0:T(8,128)(2,1)} %param.12) | copy-start | bytes 12582916
  293.7 9.4 %copy-start = (bf16[2,256,4096]{2,1,0:T(8,128)(2,1)S(1)}, bf16[2,256,4096]{2,1,0:T(8,128)(2,1)}, u32[]{:S(2)}) copy-start(bf16[2,256,4096]{2,1,0:T(8,128)(2,1)} %param.11) | copy-start | bytes 12582916
  343.6 121.7 %all-to-all-start.2 = ((bf16[8,160,4096]{2,1,0:T(8,128)(2,1)}), bf16[8,160,4096]{2,1,0:T(8,128)(2,1)}, u32[]{:S(2)}, u32[]{:S(2)}) async-start(bf16[8,160,4096]{2,1,0:T(8,128)(2,1)} %bitcast.84), calls=%async_computation.2 | async-start | bytes 20971520 | tf_op jit(solution)/shard_map/all_to_all | solution.py:69
  348.8 188.7 %reduce-scatter.2.cloned.1.call-start = ((), (), s32[]{:S(2)}) async-start(), calls=%async_computation.6 | async-start | bytes 2621440 | tf_op jit(solution)/shard_map/reduce_scatter | solution.py:79
  505.3 9.5 %copy-start.3 = (f32[8,2,80,256]{3,2,0,1:T(8,128)S(1)}, f32[8,2,80,256]{3,2,0,1:T(8,128)}, u32[]{:S(2)}) copy-start(f32[8,2,80,256]{3,2,0,1:T(8,128)} %fusion.31) | copy-start | bytes 3932164
  505.3 9.5 %copy-start.4 = (f32[8,2,80,256]{3,2,0,1:T(8,128)S(1)}, f32[8,2,80,256]{3,2,0,1:T(8,128)}, u32[]{:S(2)}) copy-start(f32[8,2,80,256]{3,2,0,1:T(8,128)} %fusion.26) | copy-start | bytes 3932164
Sparse Core Ops, SparseCore 0:
  9.5 30.6 all-gather.4
  57.6 27.7 all-gather.2
  496.2 41.2 reduce-scatter.1
where the time goes:
time: 550 us; the launch traced here: 546 us
  waiting for transfers between devices  329 us (60%)
  matrix products  86.5 us (16%)
  local copies, waits for them, and re-layouts  76.4 us (14%)
  other arithmetic  24.4 us (4%)
  starting transfers between devices  15.9 us (3%)
  between operations  14.2 us (3%)
    all_to_all x1, waiting for transfers between devices, body(): lax.all_to_all(partial_value.reshape(expert_devices, local_experts * capa...  116 us
    all_to_all x1, waiting for transfers between devices, body(): lax.all_to_all(sent_dy, 'expert', split_axis=0, concat_axis=0, tiled=True)  98.9 us
    all_to_all x1, waiting for transfers between devices, body(): lax.all_to_all(sent_x, 'expert', split_axis=0, concat_axis=0, tiled=True)  48.5 us
    all_gather x1, waiting for transfers between devices, body(): lax.all_gather(grad_out, 'edata', axis=1, tiled=True)  29.2 us
    gather x1, local copies, waits for them, and re-layouts, body(): padded_s[sender].reshape(expert_devices, local_experts * capacity, width)  23.2 us
    dot_general x1, matrix products, body(): jnp.einsum('sxcf,xfd->sxcd', up_grad, w_up, preferred_element_type=jnp.fl...  22.6 us
    all_gather x1, waiting for transfers between devices, body(): lax.all_gather(tokens, 'edata', axis=1, tiled=True)  21.1 us
    gather x1, local copies, waits for them, and re-layouts, body(): picked = returned.reshape(experts_all * capacity, width)[target]  20.4 us
  transfers between devices with their start and end apart: 6, of which 6 were waited for; matrix products, arithmetic and copies ran while one was open for 17% of the time, Pallas kernels for 0%

commit v1 on v0

--- a/solution.py
+++ b/solution.py
@@ -4,14 +4,10 @@
 from jax.sharding import PartitionSpec as P
 
 
-def body(tokens, grad_out, expert_ids, route_prob, w_gate, w_up, w_down):
-    token_count, top_count = expert_ids.shape
-    local_experts = w_gate.shape[0]
-    expert_devices = lax.axis_size("expert")
-    experts_all = expert_devices * local_experts
-    capacity = token_count * top_count * 5 // (4 * experts_all)
+def block_senders(ids, experts_all, capacity):
+    token_count, top_count = ids.shape
     pair_count = token_count * top_count
-    flat_ids = expert_ids.reshape(pair_count)
+    flat_ids = ids.reshape(pair_count)
     onehot = (flat_ids[:, None] == jnp.arange(experts_all, dtype=jnp.int32)[None, :]).astype(
         jnp.int32
     )
@@ -20,28 +16,40 @@
     target = flat_ids * capacity + slots
     sender = jnp.full((experts_all * capacity,), pair_count, jnp.int32)
     sender = sender.at[target].set(jnp.arange(pair_count, dtype=jnp.int32))
-    token_of = sender // top_count
-    whole_x, whole_dy = (
-        lax.all_gather(tokens, "edata", axis=1, tiled=True),
-        lax.all_gather(grad_out, "edata", axis=1, tiled=True),
+    return target, sender
+
+
+def body(tokens, grad_out, expert_ids, route_prob, w_gate, w_up, w_down):
+    token_count, top_count = expert_ids.shape
+    local_experts = w_gate.shape[0]
+    expert_devices = lax.axis_size("expert")
+    me = lax.axis_index("expert")
+    experts_all = expert_devices * local_experts
+    capacity = token_count * top_count * 5 // (4 * experts_all)
+    pair_count = token_count * top_count
+    target, _ = block_senders(expert_ids, experts_all, capacity)
+    all_ids = lax.all_gather(expert_ids, "expert", axis=0, tiled=False)
+    all_prob = lax.all_gather(route_prob, "expert", axis=0, tiled=False)
+    _, senders = jax.vmap(lambda i: block_senders(i, experts_all, capacity))(all_ids)
+    mine = lax.dynamic_slice_in_dim(senders, me * local_experts * capacity, local_experts * capacity, 1)
+    valid = mine < pair_count
+    source = jnp.arange(expert_devices, dtype=jnp.int32)[:, None]
+    total_tokens = expert_devices * token_count
+    token_of = jnp.where(valid, source * token_count + mine // top_count, total_tokens).reshape(-1)
+    flat_prob = jnp.concatenate(
+        [all_prob.reshape(expert_devices, pair_count), jnp.zeros((expert_devices, 1), jnp.float32)], 1
     )
-    width = whole_x.shape[1]
-    padded_x = jnp.concatenate([whole_x, jnp.zeros((1, width), jnp.bfloat16)], 0)
-    scaled = (
-        (route_prob[:, :, None] * whole_dy[:, None, :])
-        .astype(jnp.bfloat16)
-        .reshape(pair_count, width)
-    )
-    padded_s = jnp.concatenate([scaled, jnp.zeros((1, width), jnp.bfloat16)], 0)
-    sent_x = padded_x[token_of].reshape(expert_devices, local_experts * capacity, width)
-    sent_dy = padded_s[sender].reshape(expert_devices, local_experts * capacity, width)
-    sent_x, sent_dy = (sent_x, sent_dy)
-    recv_x, recv_dy = (
-        lax.all_to_all(sent_x, "expert", split_axis=0, concat_axis=0, tiled=True),
-        lax.all_to_all(sent_dy, "expert", split_axis=0, concat_axis=0, tiled=True),
-    )
-    slot_x = recv_x.reshape(expert_devices, local_experts, capacity, -1)
-    slot_dy = recv_dy.reshape(expert_devices, local_experts, capacity, -1)
+    prob_of = jnp.take_along_axis(flat_prob, jnp.minimum(mine, pair_count), 1).reshape(-1)
+    whole_x = lax.all_gather(tokens, "edata", axis=1, tiled=True)
+    whole_dy = lax.all_gather(grad_out, "edata", axis=1, tiled=True)
+    all_x = lax.all_gather(whole_x, "expert", axis=0, tiled=True)
+    all_dy = lax.all_gather(whole_dy, "expert", axis=0, tiled=True)
+    width = all_x.shape[1]
+    padded_x = jnp.concatenate([all_x, jnp.zeros((1, width), jnp.bfloat16)], 0)
+    padded_dy = jnp.concatenate([all_dy, jnp.zeros((1, width), jnp.bfloat16)], 0)
+    slot_x = padded_x[token_of].reshape(expert_devices, local_experts, capacity, width)
+    slot_dy = (prob_of[:, None] * padded_dy[token_of].astype(jnp.float32)).astype(jnp.bfloat16)
+    slot_dy = slot_dy.reshape(expert_devices, local_experts, capacity, width)
     gate_value = jnp.einsum("sxcd,xfd->sxcf", slot_x, w_gate, preferred_element_type=jnp.float32)
     up_value = jnp.einsum("sxcd,xfd->sxcf", slot_x, w_up, preferred_element_type=jnp.float32)
     sigma = jax.nn.sigmoid(gate_value)

time: 550 us -> 496 us (0.902)
  waiting for transfers between devices: 329 us -> 190 us
  local copies, waits for them, and re-layouts: 76.4 us -> 134 us
  other arithmetic: 24.4 us -> 54 us
  blocking collectives: 0 us -> 18.3 us
  matrix products: 86.5 us -> 71 us
  starting transfers between devices: 15.9 us -> 5.47 us
    all_to_all x2 -> x0, waiting for transfers between devices: 147 us -> none  [the longest x1 98.9 us: body(): lax.all_to_all(sent_dy, 'expert', split_axis=0, concat_axis=0, tiled=True)]
    another operation x3 -> x6, other arithmetic: 4.63 us -> 41.1 us
    unnamed x12 -> x24, local copies, waits for them, and re-layouts: 0.91 us -> 30.6 us
    gather x2 -> x5, local copies, waits for them, and re-layouts: 31.5 us -> 55 us  [the longest x1 23.5 us: body(): padded_dy[token_of].astype(jnp.float32)]
    all_gather x0 -> x2, blocking collectives: none -> 18.3 us  [the longest x1 9.2 us: body(): all_ids = lax.all_gather(expert_ids, 'expert', axis=0, tiled=False)]
    all_to_all x2 -> x0, starting transfers between devices: 10.7 us -> none  [the longest x1 5.41 us: body(): lax.all_to_all(sent_dy, 'expert', split_axis=0, concat_axis=0, tiled=True)]
    all_gather x2 -> x4, waiting for transfers between devices: 50.4 us -> 60.5 us  [the longest x1 31.6 us: body(): whole_x = lax.all_gather(tokens, 'edata', axis=1, tiled=True)]
    dot_general x1, matrix products: 22.6 us -> 13.2 us  [body(): jnp.einsum('sxcf,xfd->sxcd', up_grad, w_up, preferred_element_type=jnp.fl...]
  transfers between devices with their start and end apart: 6 -> 6, of which waited for: 6 -> 4; matrix products, arithmetic and copies ran while one was open for 17% -> 32% of each run, Pallas kernels for 0% -> 0%
where the time goes in v1:
time: 496 us; the launch traced here: 487 us
  waiting for transfers between devices  190 us (38%)
  local copies, waits for them, and re-layouts  134 us (27%)
  matrix products  71 us (14%)
  other arithmetic  54 us (11%)
  blocking collectives  18.3 us (4%)
  between operations  14.4 us (3%)
  starting transfers between devices  5.47 us (1%)
    all_to_all x1, waiting for transfers between devices, body(): lax.all_to_all(partial_value.reshape(expert_devices, local_experts * capa...  111 us
    another operation x6, other arithmetic  41.1 us
    all_gather x1, waiting for transfers between devices, body(): whole_x = lax.all_gather(tokens, 'edata', axis=1, tiled=True)  31.6 us
    unnamed x24, local copies, waits for them, and re-layouts  30.6 us
    all_gather x1, waiting for transfers between devices, body(): whole_dy = lax.all_gather(grad_out, 'edata', axis=1, tiled=True)  28.9 us
    gather x1, local copies, waits for them, and re-layouts, body(): padded_dy[token_of].astype(jnp.float32)  23.5 us
    gather x1, local copies, waits for them, and re-layouts, body(): padded_x[token_of].reshape(expert_devices, local_experts, capacity, width)  23.5 us
    gather x1, local copies, waits for them, and re-layouts, body(): picked = returned.reshape(experts_all * capacity, width)[target]  20.5 us
  transfers between devices with their start and end apart: 6, of which 4 were waited for; matrix products, arithmetic and copies ran while one was open for 32% of the time, Pallas kernels for 0%

profile of v1, /device:TPU:0, one launch (start us, length us, event | category | flops | bytes accessed | tf_op | source)
XLA Modules:
  0.0 487.4 jit_solution(11775011408081357752)
XLA Ops:
  7.2 0.7 all-gather.11.cloned.1.call-update
  8.0 0.7 all-gather.7.cloned.1.call-update
  8.7 31.6 %all-gather.11.cloned.1.call-done = bf16[128,4096]{1,0:T(8,128)(2,1)} async-done(((bf16[128,1024]{1,0:T(8,128)(2,1)}), bf16[128,4096]{1,0:T(8,128)(2,1)}) %all-gather.11.cloned.1.call-update) | async-done | bytes 1048592 | tf_op jit(solution)/shard_map/all_gather | solution.py:43
  40.4 28.9 %all-gather.7.cloned.1.call-done = bf16[128,4096]{1,0:T(8,128)(2,1)} async-done(((bf16[128,1024]{1,0:T(8,128)(2,1)}), bf16[128,4096]{1,0:T(8,128)(2,1)}) %all-gather.7.cloned.1.call-update) | async-done | bytes 1048592 | tf_op jit(solution)/shard_map/all_gather | solution.py:44
  69.3 9.2 %all-gather = s32[1024,8]{0,1:T(8,128)S(1)} all-gather(s32[128,8]{0,1:T(8,128)} %param.9), channel_id=2, replica_groups=mesh['edata'=4,'expert'=8] {'expert'}, dimensions={0}, use_global_device_ids=true | all-gather | bytes 36864 | tf_op jit(solution)/shard_map/all_gather | solution.py:31
  78.5 0.2 copy.19
  78.7 0.3 eq.54
  78.9 0.3 eq.50
  79.3 36.0 %reduce-window.14 = s32[8,16,8,128]{3,2,1,0:T(8,128)S(1)} reduce-window(s32[8,16,8,128]{3,2,1,0:T(8,128)S(1)} %fusion.41, s32[]{:T(128)} %constant.25.clone.1), window={size=1x1x1x128 pad=0_0x0_0x0_0x127_0}, to_apply=%region_0.0 | reduce-window | flops 16646144 | bytes 1048580 | tf_op jit(solution)/shard_map/reduce-window
  115.3 9.1 %all-gather.1 = f32[1024,8]{0,1:T(8,128)S(1)} all-gather(f32[128,8]{0,1:T(8,128)} %param.10), channel_id=3, replica_groups=mesh['edata'=4,'expert'=8] {'expert'}, dimensions={0}, use_global_device_ids=true | all-gather | bytes 36864 | tf_op jit(solution)/shard_map/all_gather | solution.py:32
  124.4 0.2 copy.23
  124.6 0.3 reshape.177
  124.9 0.2 copy.18
  125.1 0.3 mul.82
  125.3 0.2 slice.24
  125.5 0.5 copy.21
  126.1 0.2 broadcast_add_fusion
  126.4 0.1 reduce_window_sum.31
  126.5 0.1 fusion.40
  126.9 30.5 %scatter_custom_fusion = s32[10240]{0:T(1024)S(1)} fusion(s32[8192]{0:T(1024)S(1)} %get-tuple-element.7, s32[8192]{0:T(1024)S(1)} %get-tuple-element.6, s32[]{:T(128)} %constant.22.clone.1), kind=kCustom, calls=%fused_computation.63 | custom fusion | bytes 40964
  157.7 7.8 %gather_fusion.3 = f32[1280]{0:T(1024)S(1)} fusion(f32[8,1025]{1,0:T(8,128)S(1)} %concatenate.9, s32[1280]{0:T(1024)S(1)} %reshape.214), kind=kCustom, calls=%fused_computation.3 | custom fusion | bytes 20480 | tf_op jit(solution)/shard_map/jit(take_along_axis)/gather | solution.py:42
  165.8 7.8 %concatenate.11 = bf16[1025,4096]{1,0:T(8,128)(2,1)} pad(bf16[1024,4096]{1,0:T(8,128)(2,1)} %all-gather.13.cloned.1.call-done, bf16[]{:T(256)} %constant.35.clone.1), padding=0_1x0_0 | pad | bytes 16785410 | tf_op jit(solution)/shard_map/concatenate | solution.py:48
  173.6 23.5 %gather_fusion.1 = bf16[1280,4096]{1,0:T(8,128)(2,1)} fusion(bf16[1025,4096]{1,0:T(8,128)(2,1)} %concatenate.11, s32[2048]{0:T(1024)S(1)} %pad_clamp_fusion), kind=kCustom, calls=%fused_computation.1 | custom fusion | bytes 20976640 | tf_op jit(solution)/shard_map/gather | solution.py:50
  197.1 9.3 %fusion.33 = f32[8,2,80,256]{3,2,0,1:T(8,128)} fusion(bf16[2,256,4096]{2,1,0:T(8,128)(2,1)} %param.11, bf16[8,2,80,4096]{3,2,1,0:T(8,128)(2,1)} %bitcast.103), kind=kOutput, calls=%fused_computation.30 | convolution fusion | flops 2684354560 | bytes 15990784 | tf_op jit(solution)/shard_map/sxcd,xfd->sxcf/dot_general | solution.py:53
  206.4 6.1 %fusion.28 = f32[8,2,80,256]{3,2,0,1:T(8,128)} fusion(bf16[2,256,4096]{2,1,0:T(8,128)(2,1)} %param.12, bf16[8,2,80,4096]{3,2,1,0:T(8,128)(2,1)S(1)} %bitcast.105), kind=kOutput, calls=%fused_computation.29 | convolution fusion | flops 2684354560 | bytes 15990784 | tf_op jit(solution)/shard_map/sxcd,xfd->sxcf/dot_general | solution.py:54
  212.5 7.7 %concatenate.10 = bf16[1025,4096]{1,0:T(8,128)(2,1)} pad(bf16[1024,4096]{1,0:T(8,128)(2,1)} %all-gather.9.cloned.1.call-done, bf16[]{:T(256)} %constant.35.clone.1), padding=0_1x0_0 | pad | bytes 16785410 | tf_op jit(solution)/shard_map/concatenate | solution.py:49
  220.3 23.5 %gather_fusion = bf16[1280,4096]{1,0:T(8,128)(2,1)} fusion(bf16[1025,4096]{1,0:T(8,128)(2,1)} %concatenate.10, s32[2048]{0:T(1024)S(1)} %pad_clamp_fusion), kind=kCustom, calls=%fused_computation | custom fusion | bytes 20976640 | tf_op jit(solution)/shard_map/gather | solution.py:51
  243.8 9.4 %multiply_convert_fusion.1 = (bf16[8,2,80,256]{3,2,0,1:T(8,128)(2,1)S(1)}, bf16[8,2,80,256]{3,2,0,1:T(8,128)(2,1)S(1)}) fusion(f32[8,2,80,256]{3,2,0,1:T(8,128)} %fusion.33, f32[8,2,80,256]{3,2,0,1:T(8,128)} %fusion.28, bf16[2,256,4096]{2,1,0:T(8,128)(2,1)} %param.13, f32[8,2,80]{2,0,1:T(8,128)S(1)} %copy.24, bf16[8,2,80,4096]{3,2,1,0:T(8,128)(2,1)} %bitcast.109), kind=kOutput, calls=%fused_computation.32 | convolution fusion | flops 2704343040 | bytes 18617344 | tf_op jit(solution)/shard_map/sxcd,xfd->sxcf/dot_general | solution.py:58
  253.2 8.5 %fusion.14 = f32[2,8,80,4096]{3,2,1,0:T(8,128)} fusion(bf16[8,2,80,256]{3,2,0,1:T(8,128)(2,1)S(1)} %get-tuple-element.5, bf16[2,256,4096]{2,1,0:T(8,128)(2,1)S(1)} %copy-done.1), kind=kOutput, calls=%fused_computation.21 | convolution fusion | flops 2684354560 | bytes 25821184 | tf_op jit(solution)/shard_map/sxcf,xfd->sxcd/dot_general | solution.py:70
  261.8 13.2 %fusion.1 = bf16[8,2,80,4096]{3,2,0,1:T(8,128)(2,1)} fusion(f32[2,8,80,4096]{3,2,1,0:T(8,128)} %fusion.14, bf16[8,2,80,256]{3,2,0,1:T(8,128)(2,1)S(1)} %get-tuple-element.4, bf16[2,256,4096]{2,1,0:T(8,128)(2,1)} %param.12), kind=kOutput, calls=%fused_computation.9 | convolution fusion | flops 2694840320 | bytes 36306944 | tf_op jit(solution)/shard_map/sxcf,xfd->sxcd/dot_general | solution.py:73
  275.0 9.5 %copy.28 = bf16[8,2,80,4096]{3,2,1,0:T(8,128)(2,1)} copy(bf16[8,2,80,4096]{3,2,0,1:T(8,128)(2,1)} %fusion.1) | data formatting | bytes 20971520 | tf_op jit(solution)/shard_map/convert_element_type | solution.py:76
  284.4 5.3 %all-to-all-start = ((bf16[8,160,4096]{2,1,0:T(8,128)(2,1)}), bf16[8,160,4096]{2,1,0:T(8,128)(2,1)}, u32[]{:S(2)}, u32[]{:S(2)}) async-start(bf16[8,160,4096]{2,1,0:T(8,128)(2,1)} %bitcast.102), calls=%async_computation | async-start | bytes 20971520 | tf_op jit(solution)/shard_map/all_to_all | solution.py:77
  289.8 0.1 copy.30
  289.9 0.1 eq.62
  290.0 0.1 eq.58
  290.1 0.1 copy.29
  290.2 0.1 mul.96
  290.3 4.7 reduce-window.16
  295.0 0.1 copy.32
  295.3 0.1 broadcast_add_fusion.1
  295.4 110.8 %all-to-all-done = bf16[8,160,4096]{2,1,0:T(8,128)(2,1)} async-done(((bf16[8,160,4096]{2,1,0:T(8,128)(2,1)}), bf16[8,160,4096]{2,1,0:T(8,128)(2,1)}, u32[]{:S(2)}, u32[]{:S(2)}) %all-to-all-start) | async-done | bytes 10485792 | tf_op jit(solution)/shard_map/all_to_all | solution.py:77
  406.2 20.5 %gather_fusion.2 = bf16[1024,4096]{1,0:T(8,128)(2,1)} fusion(bf16[1280,4096]{1,0:T(8,128)(2,1)} %bitcast.18, s32[1024]{0:T(1024)S(1)} %broadcast_clamp_fusion), kind=kCustom, calls=%fused_computation.2 | custom fusion | bytes 16781312 | tf_op jit(solution)/shard_map/gather | solution.py:85
  426.7 10.5 %convert_reduce_fusion = f32[128,4096]{1,0:T(8,128)} fusion(bf16[1024,4096]{1,0:T(8,128)(2,1)} %gather_fusion.2), kind=kLoop, calls=%fused_computation.8 | loop fusion | flops 7864320 | bytes 10485760 | tf_op jit(solution)/shard_map/reduce_sum | solution.py:86
  437.2 9.3 %bitcast_convert_fusion.1 = bf16[2,256,4096]{2,1,0:T(8,128)(2,1)} fusion(bf16[8,2,80,256]{3,2,0,1:T(8,128)(2,1)S(1)} %get-tuple-element.4, bf16[8,2,80,4096]{3,2,1,0:T(8,128)(2,1)} %bitcast.104), kind=kOutput, calls=%fused_computation.11 | convolution fusion | flops 2686451712 | bytes 15335424 | tf_op jit(solution)/shard_map/sxcf,sxcd->xfd/dot_general | solution.py:64
  446.5 5.3 %bitcast_convert_fusion.2 = bf16[2,256,4096]{2,1,0:T(8,128)(2,1)} fusion(bf16[8,2,80,256]{3,2,0,1:T(8,128)(2,1)S(1)} %get-tuple-element.5, bf16[8,2,80,4096]{3,2,1,0:T(8,128)(2,1)S(1)} %bitcast.108), kind=kOutput, calls=%fused_computation.12 | convolution fusion | flops 2686451712 | bytes 15335424 | tf_op jit(solution)/shard_map/sxcf,sxcd->xfd/dot_general | solution.py:61
  451.8 9.9 %bitcast_convert_fusion = bf16[2,256,4096]{2,1,0:T(8,128)(2,1)} fusion(f32[8,2,80]{2,0,1:T(8,128)S(1)} %copy.24, f32[8,2,80,256]{3,2,0,1:T(8,128)S(1)} %copy-done.6, f32[8,2,80,256]{3,2,0,1:T(8,128)S(1)} %copy-done.5, bf16[8,2,80,4096]{3,2,1,0:T(8,128)(2,1)} %bitcast.110), kind=kOutput, calls=%fused_computation.10 | convolution fusion | flops 2704146432 | bytes 17306624 | tf_op jit(solution)/shard_map/sxcf,sxcd->xfd/dot_general | solution.py:67
  461.8 17.1 %reduce-scatter.2.cloned.1.call-done = f32[128,1024]{1,0:T(8,128)} async-done(((f32[128,4096]{1,0:T(8,128)}), f32[128,1024]{1,0:T(8,128)}) %reduce-scatter.2.cloned.1.call-update) | async-done | bytes 524304 | tf_op jit(solution)/shard_map/reduce_scatter | solution.py:87
  478.8 1.8 convert_element_type.71
  (65 shorter events, 1.5 us)
Async XLA Ops:
  7.2 119.5 %copy-start.4 = (s32[2]{0:T(128)S(1)}, s32[2]{0:T(128)}, u32[]{:S(2)}) copy-start(s32[2]{0:T(128)} %constant.80) | copy-start | bytes 28
  7.2 119.6 %copy-start.3 = (s32[2]{0:T(128)S(1)}, s32[2]{0:T(128)}, u32[]{:S(2)}) copy-start(s32[2]{0:T(128)} %constant.83) | copy-start | bytes 28
  7.2 33.1 %all-gather.11.cloned.1.call-start = ((), (), s32[]{:S(2)}) async-start(), calls=%async_computation.4 | async-start | bytes 1310720 | tf_op jit(solution)/shard_map/all_gather | solution.py:43
  7.9 61.3 %all-gather.7.cloned.1.call-start = ((), (), s32[]{:S(2)}) async-start(), calls=%async_computation.2 | async-start | bytes 1310720 | tf_op jit(solution)/shard_map/all_gather | solution.py:44
  8.7 157.1 %all-gather.13.cloned.1.call-start = ((), (), s32[]{:S(2)}) async-start(), calls=%async_computation.5 | async-start | bytes 9437184 | tf_op jit(solution)/shard_map/all_gather | solution.py:45
  40.3 172.2 %all-gather.9.cloned.1.call-start = ((), (), s32[]{:S(2)}) async-start(), calls=%async_computation.3 | async-start | bytes 9437184 | tf_op jit(solution)/shard_map/all_gather | solution.py:46
  197.1 9.3 %copy-start = (bf16[1280,4096]{1,0:T(8,128)(2,1)S(1)}, bf16[1280,4096]{1,0:T(8,128)(2,1)}, u32[]{:S(2)}) copy-start(bf16[1280,4096]{1,0:T(8,128)(2,1)} %gather_fusion.1) | copy-start | bytes 31457284
  243.8 9.4 %copy-start.1 = (bf16[2,256,4096]{2,1,0:T(8,128)(2,1)S(1)}, bf16[2,256,4096]{2,1,0:T(8,128)(2,1)}, u32[]{:S(2)}) copy-start(bf16[2,256,4096]{2,1,0:T(8,128)(2,1)} %param.11) | copy-start | bytes 12582916
  284.4 5.3 %copy-start.2 = (s32[128,8]{0,1:T(8,128)S(1)}, s32[128,8]{0,1:T(8,128)}, u32[]{:S(2)}) copy-start(s32[128,8]{0,1:T(8,128)} %param.9) | copy-start | bytes 12292
  284.4 121.8 %all-to-all-start = ((bf16[8,160,4096]{2,1,0:T(8,128)(2,1)}), bf16[8,160,4096]{2,1,0:T(8,128)(2,1)}, u32[]{:S(2)}, u32[]{:S(2)}) async-start(bf16[8,160,4096]{2,1,0:T(8,128)(2,1)} %bitcast.102), calls=%async_computation | async-start | bytes 20971520 | tf_op jit(solution)/shard_map/all_to_all | solution.py:77
  289.7 189.1 %reduce-scatter.2.cloned.1.call-start = ((), (), s32[]{:S(2)}) async-start(), calls=%async_computation.6 | async-start | bytes 2621440 | tf_op jit(solution)/shard_map/reduce_scatter | solution.py:87
  426.7 19.8 %slice-start = ((s8[10485760]{0:T(1024)(128)(4,1)}), s8[2097152]{0:T(1024)(128)(4,1)S(1)}, s32[]{:S(2)}) async-start(s8[10485760]{0:T(1024)(128)(4,1)} %bitcast.106), calls=%async_computation.7 | async-start | bytes 4194304
  437.2 9.3 %slice-start.1 = ((s8[10485760]{0:T(1024)(128)(4,1)}), s8[4194304]{0:T(1024)(128)(4,1)S(1)}, s32[]{:S(2)}) async-start(s8[10485760]{0:T(1024)(128)(4,1)} %bitcast.106), calls=%async_computation.8 | async-start | bytes 8388608
  437.2 9.3 %slice-start.2 = ((s8[10485760]{0:T(1024)(128)(4,1)}), s8[4194304]{0:T(1024)(128)(4,1)S(1)}, s32[]{:S(2)}) async-start(s8[10485760]{0:T(1024)(128)(4,1)} %bitcast.106), calls=%async_computation.9 | async-start | bytes 8388608
  446.5 5.3 %copy-start.5 = (f32[8,2,80,256]{3,2,0,1:T(8,128)S(1)}, f32[8,2,80,256]{3,2,0,1:T(8,128)}, u32[]{:S(2)}) copy-start(f32[8,2,80,256]{3,2,0,1:T(8,128)} %fusion.33) | copy-start | bytes 3932164
  446.5 5.3 %copy-start.6 = (f32[8,2,80,256]{3,2,0,1:T(8,128)S(1)}, f32[8,2,80,256]{3,2,0,1:T(8,128)}, u32[]{:S(2)}) copy-start(f32[8,2,80,256]{3,2,0,1:T(8,128)} %fusion.28) | copy-start | bytes 3932164
Sparse Core Ops, SparseCore 0:
  9.6 30.6 all-gather.10
  41.9 27.3 all-gather.6
  71.2 53.8 all-gather.12
  126.8 54.1 all-gather.8
  437.3 41.4 reduce-scatter.1

commit v2 on v1

v2 whole, which is shorter than its diff:
```python
import jax
import jax.numpy as jnp
from jax import lax
from jax.sharding import PartitionSpec as P


def ranks(onehot):
    pair_count = onehot.shape[-2]
    row = lax.broadcasted_iota(jnp.int32, (pair_count, pair_count), 0)
    col = lax.broadcasted_iota(jnp.int32, (pair_count, pair_count), 1)
    tri = (col < row).astype(jnp.bfloat16)
    earlier = jnp.einsum(
        "pq,...qe->...pe", tri, onehot.astype(jnp.bfloat16), preferred_element_type=jnp.float32
    )
    return earlier.astype(jnp.int32)


def body(tokens, grad_out, expert_ids, route_prob, w_gate, w_up, w_down):
    token_count, top_count = expert_ids.shape
    local_experts = w_gate.shape[0]
    expert_devices = lax.axis_size("expert")
    me = lax.axis_index("expert")
    experts_all = expert_devices * local_experts
    capacity = token_count * top_count * 5 // (4 * experts_all)
    pair_count = token_count * top_count
    cap_iota = jnp.arange(capacity, dtype=jnp.int32)

    all_ids = lax.all_gather(expert_ids, "expert", axis=0, tiled=False)
    all_prob = lax.all_gather(route_prob, "expert", axis=0, tiled=False)
    mine = me * local_experts + jnp.arange(local_experts, dtype=jnp.int32)
    named = all_ids.reshape(expert_devices, pair_count)[:, :, None] == mine
    rank = ranks(named)
    hit = named[..., None] & (rank[..., None] == cap_iota)
    hit = hit.reshape(expert_devices, token_count, top_count, local_experts, capacity)
    pick = jnp.sum(hit.astype(jnp.int32), 2).astype(jnp.bfloat16)
    prob_of = jnp.sum(jnp.where(hit, all_prob[:, :, :, None, None], 0.0), (1, 2))

    whole_x = lax.all_gather(tokens, "edata", axis=1, tiled=True)
    whole_dy = lax.all_gather(grad_out, "edata", axis=1, tiled=True)
    all_x = lax.all_gather(whole_x, "expert", axis=0, tiled=False)
    all_dy = lax.all_gather(whole_dy, "expert", axis=0, tiled=False)
    slot_x = jnp.einsum(
        "stxc,std->sxcd", pick, all_x, preferred_element_type=jnp.float32
    ).astype(jnp.bfloat16)
    slot_dy = jnp.einsum("stxc,std->sxcd", pick, all_dy, preferred_element_type=jnp.float32)
    slot_dy = (prob_of[..., None] * slot_dy).astype(jnp.bfloat16)

    gate_value = jnp.einsum("sxcd,xfd->sxcf", slot_x, w_gate, preferred_element_type=jnp.float32)
    up_value = jnp.einsum("sxcd,xfd->sxcf", slot_x, w_up, preferred_element_type=jnp.float32)
    sigma = jax.nn.sigmoid(gate_value)
    active = gate_value * sigma
    hidden = (active * up_value).astype(jnp.bfloat16)
    back = jnp.einsum("sxcd,xfd->sxcf", slot_dy, w_down, preferred_element_type=jnp.float32)
    gate_grad = (back * up_value * sigma * (1.0 + gate_value * (1.0 - sigma))).astype(jnp.bfloat16)
    up_grad = (back * active).astype(jnp.bfloat16)
    grad_gate = jnp.einsum(
        "sxcf,sxcd->xfd", gate_grad, slot_x, preferred_element_type=jnp.float32
    ).astype(jnp.bfloat16)
    grad_up = jnp.einsum(
        "sxcf,sxcd->xfd", up_grad, slot_x, preferred_element_type=jnp.float32
    ).astype(jnp.bfloat16)
    grad_down = jnp.einsum(
        "sxcf,sxcd->xfd", hidden, slot_dy, preferred_element_type=jnp.float32
    ).astype(jnp.bfloat16)
    partial_value = jnp.einsum(
        "sxcf,xfd->sxcd", gate_grad, w_gate, preferred_element_type=jnp.float32
    )
    partial_value = partial_value + jnp.einsum(
        "sxcf,xfd->sxcd", up_grad, w_up, preferred_element_type=jnp.float32
    )
    partial_value = partial_value.astype(jnp.bfloat16)
    returned = lax.all_to_all(
        partial_value.reshape(expert_devices, local_experts * capacity, -1),
        "expert",
        split_axis=0,
        concat_axis=0,
        tiled=True,
    )
    width = returned.shape[-1]

    own = expert_ids.reshape(pair_count, 1) == jnp.arange(experts_all, dtype=jnp.int32)
    slot = jnp.sum(jnp.where(own, ranks(own), 0), 1)
    back_hit = own[:, :, None] & (slot[:, None, None] == cap_iota)
    gather_back = jnp.sum(
        back_hit.reshape(token_count, top_count, experts_all * capacity).astype(jnp.int32), 1
    ).astype(jnp.bfloat16)
    per_token = jnp.einsum(
        "tq,qd->td",
        gather_back,
        returned.reshape(experts_all * capacity, width),
        preferred_element_type=jnp.float32,
    )
    grad_tokens = lax.psum_scatter(per_token, "edata", scatter_dimension=1, tiled=True).astype(
        jnp.bfloat16
    )
    return (grad_tokens, grad_gate, grad_up, grad_down)


def solution(mesh):
    placed = (
        P("expert", "edata"),
        P("expert", "edata"),
        P("expert", None),
        P("expert", None),
        P("expert", "edata", None),
        P("expert", "edata", None),
        P("expert", "edata", None),
    )
    return jax.shard_map(
        body,
        mesh=mesh,
        in_specs=placed,
        out_specs=(
            P("expert", "edata"),
            P("expert", "edata", None),
            P("expert", "edata", None),
            P("expert", "edata", None),
        ),
        check_vma=False,
    )
```

time: 496 us -> 412 us (0.83); the launches traced: 487 us -> 411 us
  local copies, waits for them, and re-layouts: 134 us -> 20.4 us
  waiting for transfers between devices: 190 us -> 242 us
  other arithmetic: 54 us -> 16.3 us
  matrix products: 71 us -> 94.8 us
    gather x6 -> x0, local copies, waits for them, and re-layouts: 75.5 us -> none  [the longest x1 23.5 us: body(): padded_dy[token_of].astype(jnp.float32)]
    all_gather x2, waiting for transfers between devices: 0.02 us -> 66.4 us  [the longest x1 34 us: body(): all_dy = lax.all_gather(whole_dy, 'expert', axis=0, tiled=False)]
    another operation x6 -> x0, other arithmetic: 41.1 us -> none
    unnamed x24 -> x19, local copies, waits for them, and re-layouts: 30.6 us -> 0.14 us
    dot_general x0 -> x5, matrix products: none -> 24.4 us  [the longest x1 10.3 us: body(): jnp.einsum('stxc,std->sxcd', pick, all_dy, preferred_element_type=jnp.flo...]
    all_to_all x1, waiting for transfers between devices: 111 us -> 94.4 us  [body(): lax.all_to_all(partial_value.reshape(expert_devices, local_experts * capa...]
    concatenate x3 -> x0, local copies, waits for them, and re-layouts: 15.5 us -> none  [the longest x1 7.75 us: body(): padded_x = jnp.concatenate([all_x, jnp.zeros((1, width), jnp.bfloat16)], 0)]
    convert_element_type x0 -> x1, local copies, waits for them, and re-layouts: none -> 9.07 us  [body(): back_hit.reshape(token_count, top_count, experts_all * capacity)]
  transfers between devices with their start and end apart: 6 -> 6, of which waited for: 4 -> 6; matrix products, arithmetic and copies ran while one was open for 32% -> 18% of each run, Pallas kernels for 0% -> 0%
where the time goes in v2:
time: 412 us; the launch traced here: 411 us
  waiting for transfers between devices  242 us (59%)
  matrix products  94.8 us (23%)
  local copies, waits for them, and re-layouts  20.4 us (5%)
  blocking collectives  18.6 us (5%)
  other arithmetic  16.3 us (4%)
  between operations  14 us (3%)
  starting transfers between devices  5.69 us (1%)
    all_to_all x1, waiting for transfers between devices, body(): lax.all_to_all(partial_value.reshape(expert_devices, local_experts * capa...  94.4 us
    all_gather x1, waiting for transfers between devices, body(): all_dy = lax.all_gather(whole_dy, 'expert', axis=0, tiled=False)  34 us
    all_gather x1, waiting for transfers between devices, body(): all_x = lax.all_gather(whole_x, 'expert', axis=0, tiled=False)  32.4 us
    all_gather x1, waiting for transfers between devices, body(): whole_x = lax.all_gather(tokens, 'edata', axis=1, tiled=True)  31.6 us
    all_gather x1, waiting for transfers between devices, body(): whole_dy = lax.all_gather(grad_out, 'edata', axis=1, tiled=True)  28.9 us
    reduce_scatter x1, waiting for transfers between devices, body(): lax.psum_scatter(per_token, 'edata', scatter_dimension=1, tiled=True)  19 us
    dot_general x1, matrix products, body(): jnp.einsum('sxcf,xfd->sxcd', up_grad, w_up, preferred_element_type=jnp.fl...  13 us
    dot_general x1, matrix products, body(): jnp.einsum('stxc,std->sxcd', pick, all_dy, preferred_element_type=jnp.flo...  10.3 us
  transfers between devices with their start and end apart: 6, of which 6 were waited for; matrix products, arithmetic and copies ran while one was open for 18% of the time, Pallas kernels for 0%

profile of v2, /device:TPU:0, one launch (start us, length us, event | category | flops | bytes accessed | tf_op | source)
XLA Modules:
  0.0 411.5 jit_solution(5290458668592354634)
XLA Ops:
  7.2 0.0 all-gather.11.cloned.1.call-start
  7.2 0.7 all-gather.11.cloned.1.call-update
  7.9 0.0 all-gather.9.cloned.1.call-start
  8.0 0.7 all-gather.9.cloned.1.call-update
  8.7 0.0 all-gather.15.cloned.1.call-start
  8.7 31.6 %all-gather.11.cloned.1.call-done = bf16[128,4096]{1,0:T(8,128)(2,1)} async-done(((bf16[128,1024]{1,0:T(8,128)(2,1)}), bf16[128,4096]{1,0:T(8,128)(2,1)}) %all-gather.11.cloned.1.call-update) | async-done | bytes 1048592 | tf_op jit(solution)/shard_map/all_gather | solution.py:38
  40.3 0.0 all-gather.15.cloned.1.call-update
  40.3 0.0 all-gather.13.cloned.1.call-start
  40.4 28.9 %all-gather.9.cloned.1.call-done = bf16[128,4096]{1,0:T(8,128)(2,1)} async-done(((bf16[128,1024]{1,0:T(8,128)(2,1)}), bf16[128,4096]{1,0:T(8,128)(2,1)}) %all-gather.9.cloned.1.call-update) | async-done | bytes 1048592 | tf_op jit(solution)/shard_map/all_gather | solution.py:39
  69.3 0.0 all-gather.13.cloned.1.call-update
  69.3 9.2 %all-gather = s32[1024,8]{0,1:T(8,128)S(1)} all-gather(s32[128,8]{0,1:T(8,128)} %param.9), channel_id=2, replica_groups=mesh['edata'=4,'expert'=8] {'expert'}, dimensions={0}, use_global_device_ids=true | all-gather | bytes 36864 | tf_op jit(solution)/shard_map/all_gather | solution.py:28
  78.5 0.2 copy.37
  78.7 0.1 broadcast_compare_fusion
  78.8 0.3 eq.88
  79.1 0.5 fusion.49
  79.6 0.6 eq.92
  80.2 0.3 copy.38
  80.5 9.4 %all-gather.1 = f32[1024,8]{0,1:T(8,128)S(1)} all-gather(f32[128,8]{0,1:T(8,128)S(1)} %copy-done.3), channel_id=3, replica_groups=mesh['edata'=4,'expert'=8] {'expert'}, dimensions={0}, use_global_device_ids=true | all-gather | bytes 36864 | tf_op jit(solution)/shard_map/all_gather | solution.py:29
  89.9 1.3 convert_reduce_fusion
  91.2 1.3 select_reduce_fusion
  92.5 32.4 %all-gather.15.cloned.1.call-done = bf16[1024,4096]{1,0:T(8,128)(2,1)} async-done(((bf16[128,4096]{1,0:T(8,128)(2,1)}), bf16[1024,4096]{1,0:T(8,128)(2,1)}) %all-gather.15.cloned.1.call-update) | async-done | bytes 8388624 | tf_op jit(solution)/shard_map/all_gather | solution.py:40
  124.9 6.3 %convolution_convert_fusion = bf16[8,2,80,4096]{3,2,1,0:T(8,128)(2,1)S(1)} fusion(bf16[8,128,4096,1]{2,1,3,0:T(8,128)(2,1)} %bitcast.79, s32[8,128,2,80]{1,3,2,0:T(8,128)S(1)} %convert_reduce_fusion), kind=kOutput, calls=%fused_computation.11 | convolution fusion | flops 1347584000 | bytes 19529728 | tf_op jit(solution)/shard_map/stxc,std->sxcd/dot_general | solution.py:42
  131.2 9.6 %fusion.35 = f32[8,2,80,256]{3,2,0,1:T(8,128)} fusion(bf16[2,256,4096]{2,1,0:T(8,128)(2,1)} %param.11, bf16[8,2,80,4096]{3,2,1,0:T(8,128)(2,1)S(1)} %convolution_convert_fusion), kind=kOutput, calls=%fused_computation.35 | convolution fusion | flops 2684354560 | bytes 15990784 | tf_op jit(solution)/shard_map/sxcd,xfd->sxcf/dot_general | solution.py:48
  140.8 6.1 %fusion.30 = f32[8,2,80,256]{3,2,0,1:T(8,128)} fusion(bf16[2,256,4096]{2,1,0:T(8,128)(2,1)} %param.12, bf16[8,2,80,4096]{3,2,1,0:T(8,128)(2,1)S(1)} %convolution_convert_fusion), kind=kOutput, calls=%fused_computation.34 | convolution fusion | flops 2684354560 | bytes 15990784 | tf_op jit(solution)/shard_map/sxcd,xfd->sxcf/dot_general | solution.py:49
  146.9 34.0 %all-gather.13.cloned.1.call-done = bf16[1024,4096]{1,0:T(8,128)(2,1)} async-done(((bf16[128,4096]{1,0:T(8,128)(2,1)}), bf16[1024,4096]{1,0:T(8,128)(2,1)}) %all-gather.13.cloned.1.call-update) | async-done | bytes 8388624 | tf_op jit(solution)/shard_map/all_gather | solution.py:41
  180.9 10.3 %multiply_convert_fusion = bf16[8,2,80,4096]{3,2,1,0:T(8,128)(2,1)} fusion(f32[8,2,80]{2,1,0:T(2,128)S(1)} %select_reduce_fusion, bf16[8,128,4096,1]{2,1,3,0:T(8,128)(2,1)} %bitcast.80, s32[8,128,2,80]{1,3,2,0:T(8,128)S(1)} %convert_reduce_fusion), kind=kOutput, calls=%fused_computation.1 | convolution fusion | flops 1352826880 | bytes 19534848 | tf_op jit(solution)/shard_map/stxc,std->sxcd/dot_general | solution.py:45
  191.3 9.4 %multiply_convert_fusion.2 = (bf16[8,2,80,256]{3,2,0,1:T(8,128)(2,1)S(1)}, bf16[8,2,80,256]{3,2,0,1:T(8,128)(2,1)S(1)}) fusion(f32[8,2,80,256]{3,2,0,1:T(8,128)} %fusion.35, f32[8,2,80,256]{3,2,0,1:T(8,128)} %fusion.30, bf16[2,256,4096]{2,1,0:T(8,128)(2,1)} %param.13, bf16[8,2,80,4096]{3,2,1,0:T(8,128)(2,1)} %multiply_convert_fusion), kind=kOutput, calls=%fused_computation.38 | convolution fusion | flops 2688614400 | bytes 18612224 | tf_op jit(solution)/shard_map/sxcd,xfd->sxcf/dot_general | solution.py:53
  200.6 8.5 %fusion.20 = f32[2,8,80,4096]{3,2,1,0:T(8,128)} fusion(bf16[8,2,80,256]{3,2,0,1:T(8,128)(2,1)S(1)} %get-tuple-element.5, bf16[2,256,4096]{2,1,0:T(8,128)(2,1)S(1)} %copy-done.1), kind=kOutput, calls=%fused_computation.24 | convolution fusion | flops 2684354560 | bytes 25821184 | tf_op jit(solution)/shard_map/sxcf,xfd->sxcd/dot_general | solution.py:65
  209.2 13.0 %fusion = bf16[8,2,80,4096]{3,2,0,1:T(8,128)(2,1)} fusion(f32[2,8,80,4096]{3,2,1,0:T(8,128)} %fusion.20, bf16[8,2,80,256]{3,2,0,1:T(8,128)(2,1)S(1)} %get-tuple-element.4, bf16[2,256,4096]{2,1,0:T(8,128)(2,1)} %param.12), kind=kOutput, calls=%fused_computation.2 | convolution fusion | flops 2694840320 | bytes 36306944 | tf_op jit(solution)/shard_map/sxcf,xfd->sxcd/dot_general | solution.py:68
  222.1 9.5 %copy.42 = bf16[8,2,80,4096]{3,2,1,0:T(8,128)(2,1)} copy(bf16[8,2,80,4096]{3,2,0,1:T(8,128)(2,1)} %fusion) | data formatting | bytes 20971520 | tf_op jit(solution)/shard_map/convert_element_type | solution.py:71
  231.6 5.3 %all-to-all-start = ((bf16[8,160,4096]{2,1,0:T(8,128)(2,1)}), bf16[8,160,4096]{2,1,0:T(8,128)(2,1)}, u32[]{:S(2)}, u32[]{:S(2)}) async-start(bf16[8,160,4096]{2,1,0:T(8,128)(2,1)} %bitcast.76), calls=%async_computation | async-start | bytes 20971520 | tf_op jit(solution)/shard_map/all_to_all | solution.py:72
  236.9 0.3 reduce-scatter.2.cloned.1.call-start
  237.2 0.1 copy.34
  237.3 0.1 eq.78
  237.4 0.3 copy.35
  237.7 0.5 fusion.54
  238.2 0.2 iota_compare_fusion.9
  238.4 7.9 %and_convert_fusion = s32[1024,16,80]{2,1,0:T(8,128)} fusion(pred[1024,80]{1,0:T(8,128)(4,1)S(1)} %iota_compare_fusion.9, pred[1024,16]{1,0:T(8,128)(4,1)S(1)} %copy.35), kind=kLoop, calls=%fused_computation.10 | loop fusion | flops 2621440 | bytes 5341184 | tf_op jit(solution)/shard_map/convert_element_type | solution.py:85
  246.2 9.1 %reshape.84 = s32[128,8,1280]{2,1,0:T(8,128)} reshape(s32[1024,16,80]{2,1,0:T(8,128)} %and_convert_fusion) | data formatting | bytes 10485760 | tf_op jit(solution)/shard_map/convert_element_type | solution.py:85
  255.3 3.7 reduce_sum.37
  259.0 94.4 %all-to-all-done = bf16[8,160,4096]{2,1,0:T(8,128)(2,1)} async-done(((bf16[8,160,4096]{2,1,0:T(8,128)(2,1)}), bf16[8,160,4096]{2,1,0:T(8,128)(2,1)}, u32[]{:S(2)}, u32[]{:S(2)}) %all-to-all-start) | async-done | bytes 10485792 | tf_op jit(solution)/shard_map/all_to_all | solution.py:72
  353.4 6.8 %fusion.55 = f32[128,4096]{1,0:T(8,128)} fusion(bf16[1280,4096]{1,0:T(8,128)(2,1)} %bitcast.22, s32[128,1280]{1,0:T(8,128)S(1)} %reduce_sum.37), kind=kOutput, calls=%fused_computation.48 | convolution fusion | flops 1342341120 | bytes 13238272 | tf_op jit(solution)/shard_map/tq,qd->td/dot_general | solution.py:87
  360.2 0.0 reduce-scatter.2.cloned.1.call-update
  360.3 9.2 %bitcast_convert_fusion.1 = bf16[2,256,4096]{2,1,0:T(8,128)(2,1)} fusion(bf16[8,2,80,256]{3,2,0,1:T(8,128)(2,1)S(1)} %get-tuple-element.4, bf16[8,2,80,4096]{3,2,1,0:T(8,128)(2,1)} %copy-done), kind=kOutput, calls=%fused_computation.8 | convolution fusion | flops 2686451712 | bytes 15335424 | tf_op jit(solution)/shard_map/sxcf,sxcd->xfd/dot_general | solution.py:59
  369.5 9.3 %bitcast_convert_fusion.2 = bf16[2,256,4096]{2,1,0:T(8,128)(2,1)} fusion(bf16[8,2,80,256]{3,2,0,1:T(8,128)(2,1)S(1)} %get-tuple-element.5, bf16[8,2,80,4096]{3,2,1,0:T(8,128)(2,1)} %copy-done), kind=kOutput, calls=%fused_computation.9 | convolution fusion | flops 2686451712 | bytes 15335424 | tf_op jit(solution)/shard_map/sxcf,sxcd->xfd/dot_general | solution.py:56
  378.8 5.3 %bitcast_convert_fusion = bf16[2,256,4096]{2,1,0:T(8,128)(2,1)} fusion(bf16[8,2,80,4096]{3,2,1,0:T(8,128)(2,1)S(1)} %bitcast.78, f32[8,2,80,256]{3,2,0,1:T(8,128)S(1)} %copy-done.5, f32[8,2,80,256]{3,2,0,1:T(8,128)S(1)} %copy-done.4), kind=kOutput, calls=%fused_computation.7 | convolution fusion | flops 2688417792 | bytes 17301504 | tf_op jit(solution)/shard_map/sxcf,sxcd->xfd/dot_general | solution.py:62
  384.2 19.0 %reduce-scatter.2.cloned.1.call-done = f32[128,1024]{1,0:T(8,128)} async-done(((f32[128,4096]{1,0:T(8,128)}), f32[128,1024]{1,0:T(8,128)}) %reduce-scatter.2.cloned.1.call-update) | async-done | bytes 524304 | tf_op jit(solution)/shard_map/reduce_scatter | solution.py:93
  403.2 1.8 convert_element_type.75
  (22 shorter events, 0.1 us)
Async XLA Ops:
  7.2 73.4 %copy-start.3 = (f32[128,8]{0,1:T(8,128)S(1)}, f32[128,8]{0,1:T(8,128)}, u32[]{:S(2)}) copy-start(f32[128,8]{0,1:T(8,128)} %param.10) | copy-start | bytes 12292
  7.2 33.1 %all-gather.11.cloned.1.call-start = ((), (), s32[]{:S(2)}) async-start(), calls=%async_computation.3 | async-start | bytes 1310720 | tf_op jit(solution)/shard_map/all_gather | solution.py:38
  7.9 61.3 %all-gather.9.cloned.1.call-start = ((), (), s32[]{:S(2)}) async-start(), calls=%async_computation.2 | async-start | bytes 1310720 | tf_op jit(solution)/shard_map/all_gather | solution.py:39
  8.7 116.2 %all-gather.15.cloned.1.call-start = ((), (), s32[]{:S(2)}) async-start(), calls=%async_computation.6 | async-start | bytes 9437184 | tf_op jit(solution)/shard_map/all_gather | solution.py:40
  40.3 140.6 %all-gather.13.cloned.1.call-start = ((), (), s32[]{:S(2)}) async-start(), calls=%async_computation.5 | async-start | bytes 9437184 | tf_op jit(solution)/shard_map/all_gather | solution.py:41
  131.2 9.6 %copy-start = (bf16[8,2,80,4096]{3,2,1,0:T(8,128)(2,1)}, bf16[8,2,80,4096]{3,2,1,0:T(8,128)(2,1)S(1)}, u32[]{:S(2)}) copy-start(bf16[8,2,80,4096]{3,2,1,0:T(8,128)(2,1)S(1)} %convolution_convert_fusion) | copy-start | bytes 31457284
  191.3 9.4 %copy-start.1 = (bf16[2,256,4096]{2,1,0:T(8,128)(2,1)S(1)}, bf16[2,256,4096]{2,1,0:T(8,128)(2,1)}, u32[]{:S(2)}) copy-start(bf16[2,256,4096]{2,1,0:T(8,128)(2,1)} %param.11) | copy-start | bytes 12582916
  231.6 5.6 %copy-start.2 = (s32[128,8]{0,1:T(8,128)S(1)}, s32[128,8]{0,1:T(8,128)}, u32[]{:S(2)}) copy-start(s32[128,8]{0,1:T(8,128)} %param.9) | copy-start | bytes 12292
  231.6 121.8 %all-to-all-start = ((bf16[8,160,4096]{2,1,0:T(8,128)(2,1)}), bf16[8,160,4096]{2,1,0:T(8,128)(2,1)}, u32[]{:S(2)}, u32[]{:S(2)}) async-start(bf16[8,160,4096]{2,1,0:T(8,128)(2,1)} %bitcast.76), calls=%async_computation | async-start | bytes 20971520 | tf_op jit(solution)/shard_map/all_to_all | solution.py:72
  236.9 166.3 %reduce-scatter.2.cloned.1.call-start = ((), (), s32[]{:S(2)}) async-start(), calls=%async_computation.4 | async-start | bytes 2621440 | tf_op jit(solution)/shard_map/reduce_scatter | solution.py:93
  360.3 18.5 %slice-start = ((s8[10485760]{0:T(1024)(128)(4,1)}), s8[4194304]{0:T(1024)(128)(4,1)S(1)}, s32[]{:S(2)}) async-start(s8[10485760]{0:T(1024)(128)(4,1)} %bitcast.77), calls=%async_computation.7 | async-start | bytes 8388608
  360.3 18.5 %slice-start.1 = ((s8[10485760]{0:T(1024)(128)(4,1)}), s8[4194304]{0:T(1024)(128)(4,1)S(1)}, s32[]{:S(2)}) async-start(s8[10485760]{0:T(1024)(128)(4,1)} %bitcast.77), calls=%async_computation.8 | async-start | bytes 8388608
  369.5 9.3 %slice-start.2 = ((s8[10485760]{0:T(1024)(128)(4,1)}), s8[2097152]{0:T(1024)(128)(4,1)S(1)}, s32[]{:S(2)}) async-start(s8[10485760]{0:T(1024)(128)(4,1)} %bitcast.77), calls=%async_computation.9 | async-start | bytes 4194304
  369.5 9.3 %copy-start.4 = (f32[8,2,80,256]{3,2,0,1:T(8,128)S(1)}, f32[8,2,80,256]{3,2,0,1:T(8,128)}, u32[]{:S(2)}) copy-start(f32[8,2,80,256]{3,2,0,1:T(8,128)} %fusion.35) | copy-start | bytes 3932164
  369.5 9.3 %copy-start.5 = (f32[8,2,80,256]{3,2,0,1:T(8,128)S(1)}, f32[8,2,80,256]{3,2,0,1:T(8,128)}, u32[]{:S(2)}) copy-start(f32[8,2,80,256]{3,2,0,1:T(8,128)} %fusion.30) | copy-start | bytes 3932164
Sparse Core Ops, SparseCore 0:
  9.6 30.6 all-gather.10
  41.9 27.3 all-gather.8
  71.1 53.7 all-gather.14
  126.6 54.2 all-gather.12
  360.4 42.7 reduce-scatter.1

commit v3 on v2

--- a/solution.py
+++ b/solution.py
@@ -35,10 +35,9 @@
     pick = jnp.sum(hit.astype(jnp.int32), 2).astype(jnp.bfloat16)
     prob_of = jnp.sum(jnp.where(hit, all_prob[:, :, :, None, None], 0.0), (1, 2))
 
-    whole_x = lax.all_gather(tokens, "edata", axis=1, tiled=True)
-    whole_dy = lax.all_gather(grad_out, "edata", axis=1, tiled=True)
-    all_x = lax.all_gather(whole_x, "expert", axis=0, tiled=False)
-    all_dy = lax.all_gather(whole_dy, "expert", axis=0, tiled=False)
+    both = lax.all_gather(jnp.stack([tokens, grad_out]), "edata", axis=2, tiled=True)
+    both = lax.all_gather(both, "expert", axis=1, tiled=False)
+    all_x, all_dy = both[0], both[1]
     slot_x = jnp.einsum(
         "stxc,std->sxcd", pick, all_x, preferred_element_type=jnp.float32
     ).astype(jnp.bfloat16)

time: 412 us -> 409 us (level)
  waiting for transfers between devices: 242 us -> 230 us
  local copies, waits for them, and re-layouts: 20.4 us -> 29.9 us
    all_gather x4 -> x2, waiting for transfers between devices: 127 us -> 117 us  [the longest x1 67.3 us: body(): both = lax.all_gather(both, 'expert', axis=1, tiled=False)]
    slice x0 -> x1, local copies, waits for them, and re-layouts: none -> 9.49 us  [body(): all_x, all_dy = (both[0], both[1])]
    dot_general x1, matrix products: 10.3 us -> 5.37 us  [body(): jnp.einsum('stxc,std->sxcd', pick, all_dy, preferred_element_type=jnp.flo...]
  transfers between devices with their start and end apart: 6 -> 4, of which waited for: 6 -> 4; matrix products, arithmetic and copies ran while one was open for 18% -> 12% of each run, Pallas kernels for 0% -> 0%
where the time goes in v3:
time: 409 us; the launch traced here: 408 us
  waiting for transfers between devices  230 us (56%)
  matrix products  92.1 us (23%)
  local copies, waits for them, and re-layouts  29.9 us (7%)
  blocking collectives  18.6 us (5%)
  other arithmetic  18.2 us (4%)
  between operations  13.9 us (3%)
  starting transfers between devices  5.41 us (1%)
    all_to_all x1, waiting for transfers between devices, body(): lax.all_to_all(partial_value.reshape(expert_devices, local_experts * capa...  94.6 us
    all_gather x1, waiting for transfers between devices, body(): both = lax.all_gather(both, 'expert', axis=1, tiled=False)  67.3 us
    all_gather x1, waiting for transfers between devices, body(): lax.all_gather(jnp.stack([tokens, grad_out]), 'edata', axis=2, tiled=True)  49.4 us
    reduce_scatter x1, waiting for transfers between devices, body(): lax.psum_scatter(per_token, 'edata', scatter_dimension=1, tiled=True)  19 us
    dot_general x1, matrix products, body(): jnp.einsum('sxcf,xfd->sxcd', up_grad, w_up, preferred_element_type=jnp.fl...  13 us
    slice x1, local copies, waits for them, and re-layouts, body(): all_x, all_dy = (both[0], both[1])  9.49 us
    convert_element_type x1, local copies, waits for them, and re-layouts, body(): partial_value = partial_value.astype(jnp.bfloat16)  9.44 us
    all_gather x1, blocking collectives, body(): all_prob = lax.all_gather(route_prob, 'expert', axis=0, tiled=False)  9.37 us
  transfers between devices with their start and end apart: 4, of which 4 were waited for; matrix products, arithmetic and copies ran while one was open for 12% of the time, Pallas kernels for 0%

profile of v3, /device:TPU:0, one launch (start us, length us, event | category | flops | bytes accessed | tf_op | source)
XLA Modules:
  0.0 408.4 jit_solution(8426110478002585306)
XLA Ops:
  7.2 0.0 all-gather.6.cloned.1.call-start
  7.2 1.9 pad_maximum_fusion
  9.1 0.0 all-gather.6.cloned.1.call-update
  9.1 0.0 all-gather.8.cloned.1.call-start
  9.2 49.4 %all-gather.6.cloned.1.call-done = bf16[2,128,4096]{2,1,0:T(8,128)(2,1)} async-done(((bf16[2,128,1024]{2,1,0:T(8,128)(2,1)}), bf16[2,128,4096]{2,1,0:T(8,128)(2,1)}) %all-gather.6.cloned.1.call-update) | async-done | bytes 2097168 | tf_op jit(solution)/shard_map/all_gather | solution.py:38
  58.5 0.0 all-gather.8.cloned.1.call-update
  58.6 9.2 %all-gather = s32[1024,8]{0,1:T(8,128)S(1)} all-gather(s32[128,8]{0,1:T(8,128)} %param.9), channel_id=2, replica_groups=mesh['edata'=4,'expert'=8] {'expert'}, dimensions={0}, use_global_device_ids=true | all-gather | bytes 36864 | tf_op jit(solution)/shard_map/all_gather | solution.py:28
  67.8 0.2 copy.37
  68.0 0.1 broadcast_compare_fusion
  68.1 0.3 eq.88
  68.4 0.5 fusion.49
  68.9 0.6 eq.92
  69.5 0.3 copy.38
  69.8 0.0 copy-done.2
  69.8 9.4 %all-gather.1 = f32[1024,8]{0,1:T(8,128)S(1)} all-gather(f32[128,8]{0,1:T(8,128)S(1)} %copy-done.2), channel_id=3, replica_groups=mesh['edata'=4,'expert'=8] {'expert'}, dimensions={0}, use_global_device_ids=true | all-gather | bytes 36864 | tf_op jit(solution)/shard_map/all_gather | solution.py:29
  79.2 1.3 convert_reduce_fusion
  80.5 1.3 select_reduce_fusion
  81.8 67.3 %all-gather.8.cloned.1.call-done = bf16[2,1024,4096]{2,1,0:T(8,128)(2,1)} async-done(((bf16[2,128,4096]{2,1,0:T(8,128)(2,1)}), bf16[2,1024,4096]{2,1,0:T(8,128)(2,1)}) %all-gather.8.cloned.1.call-update) | async-done | bytes 16777232 | tf_op jit(solution)/shard_map/all_gather | solution.py:39
  149.1 9.5 %fusion.64 = (bf16[1,1024,4096]{2,1,0:T(8,128)(2,1)}, bf16[1,1024,4096]{2,1,0:T(8,128)(2,1)S(1)}) fusion(bf16[2,1024,4096]{2,1,0:T(8,128)(2,1)} %all-gather.8.cloned.1.call-done), kind=kLoop, calls=%fused_computation.60 | loop fusion | bytes 33554432 | tf_op jit(solution)/shard_map/slice | solution.py:40
  158.6 5.5 %convolution_convert_fusion = bf16[8,2,80,4096]{3,2,1,0:T(8,128)(2,1)} fusion(bf16[8,128,4096,1]{2,1,3,0:T(8,128)(2,1)S(1)} %bitcast.79, s32[8,128,2,80]{1,3,2,0:T(8,128)S(1)} %convert_reduce_fusion), kind=kOutput, calls=%fused_computation.11 | convolution fusion | flops 1347584000 | bytes 19529728 | tf_op jit(solution)/shard_map/stxc,std->sxcd/dot_general | solution.py:41
  164.1 9.3 %fusion.35 = f32[8,2,80,256]{3,2,0,1:T(8,128)} fusion(bf16[2,256,4096]{2,1,0:T(8,128)(2,1)} %param.11, bf16[8,2,80,4096]{3,2,1,0:T(8,128)(2,1)} %convolution_convert_fusion), kind=kOutput, calls=%fused_computation.35 | convolution fusion | flops 2684354560 | bytes 15990784 | tf_op jit(solution)/shard_map/sxcd,xfd->sxcf/dot_general | solution.py:47
  173.3 9.3 %fusion.30 = f32[8,2,80,256]{3,2,0,1:T(8,128)} fusion(bf16[2,256,4096]{2,1,0:T(8,128)(2,1)} %param.12, bf16[8,2,80,4096]{3,2,1,0:T(8,128)(2,1)} %convolution_convert_fusion), kind=kOutput, calls=%fused_computation.34 | convolution fusion | flops 2684354560 | bytes 15990784 | tf_op jit(solution)/shard_map/sxcd,xfd->sxcf/dot_general | solution.py:48
  182.6 5.4 %multiply_convert_fusion = bf16[8,2,80,4096]{3,2,1,0:T(8,128)(2,1)} fusion(f32[8,2,80]{2,1,0:T(2,128)S(1)} %select_reduce_fusion, bf16[8,128,4096,1]{2,1,3,0:T(8,128)(2,1)S(1)} %bitcast.82, s32[8,128,2,80]{1,3,2,0:T(8,128)S(1)} %convert_reduce_fusion), kind=kOutput, calls=%fused_computation.1 | convolution fusion | flops 1352826880 | bytes 19534848 | tf_op jit(solution)/shard_map/stxc,std->sxcd/dot_general | solution.py:44
  188.0 9.4 %multiply_convert_fusion.2 = (bf16[8,2,80,256]{3,2,0,1:T(8,128)(2,1)S(1)}, bf16[8,2,80,256]{3,2,0,1:T(8,128)(2,1)S(1)}) fusion(f32[8,2,80,256]{3,2,0,1:T(8,128)} %fusion.35, f32[8,2,80,256]{3,2,0,1:T(8,128)} %fusion.30, bf16[2,256,4096]{2,1,0:T(8,128)(2,1)} %param.13, bf16[8,2,80,4096]{3,2,1,0:T(8,128)(2,1)} %multiply_convert_fusion), kind=kOutput, calls=%fused_computation.38 | convolution fusion | flops 2688614400 | bytes 18612224 | tf_op jit(solution)/shard_map/sxcd,xfd->sxcf/dot_general | solution.py:52
  197.4 8.7 %fusion.20 = f32[2,8,80,4096]{3,2,1,0:T(8,128)} fusion(bf16[8,2,80,256]{3,2,0,1:T(8,128)(2,1)S(1)} %get-tuple-element.7, bf16[2,256,4096]{2,1,0:T(8,128)(2,1)S(1)} %copy-done), kind=kOutput, calls=%fused_computation.24 | convolution fusion | flops 2684354560 | bytes 25821184 | tf_op jit(solution)/shard_map/sxcf,xfd->sxcd/dot_general | solution.py:64
  206.1 13.0 %fusion = bf16[8,2,80,4096]{3,2,0,1:T(8,128)(2,1)} fusion(f32[2,8,80,4096]{3,2,1,0:T(8,128)} %fusion.20, bf16[8,2,80,256]{3,2,0,1:T(8,128)(2,1)S(1)} %get-tuple-element.6, bf16[2,256,4096]{2,1,0:T(8,128)(2,1)} %param.12), kind=kOutput, calls=%fused_computation.2 | convolution fusion | flops 2694840320 | bytes 36306944 | tf_op jit(solution)/shard_map/sxcf,xfd->sxcd/dot_general | solution.py:67
  219.1 9.4 %copy.42 = bf16[8,2,80,4096]{3,2,1,0:T(8,128)(2,1)} copy(bf16[8,2,80,4096]{3,2,0,1:T(8,128)(2,1)} %fusion) | data formatting | bytes 20971520 | tf_op jit(solution)/shard_map/convert_element_type | solution.py:70
  228.5 5.3 %all-to-all-start = ((bf16[8,160,4096]{2,1,0:T(8,128)(2,1)}), bf16[8,160,4096]{2,1,0:T(8,128)(2,1)}, u32[]{:S(2)}, u32[]{:S(2)}) async-start(bf16[8,160,4096]{2,1,0:T(8,128)(2,1)} %bitcast.78), calls=%async_computation | async-start | bytes 20971520 | tf_op jit(solution)/shard_map/all_to_all | solution.py:71
  233.8 0.0 reduce-scatter.2.cloned.1.call-start
  233.9 0.1 copy.34
  234.0 0.1 eq.78
  234.1 0.3 copy.35
  234.4 0.5 fusion.54
  234.9 0.2 iota_compare_fusion.9
  235.1 7.9 %and_convert_fusion = s32[1024,16,80]{2,1,0:T(8,128)} fusion(pred[1024,80]{1,0:T(8,128)(4,1)S(1)} %iota_compare_fusion.9, pred[1024,16]{1,0:T(8,128)(4,1)S(1)} %copy.35), kind=kLoop, calls=%fused_computation.10 | loop fusion | flops 2621440 | bytes 5341184 | tf_op jit(solution)/shard_map/convert_element_type | solution.py:84
  243.0 9.1 %reshape.84 = s32[128,8,1280]{2,1,0:T(8,128)} reshape(s32[1024,16,80]{2,1,0:T(8,128)} %and_convert_fusion) | data formatting | bytes 10485760 | tf_op jit(solution)/shard_map/convert_element_type | solution.py:84
  252.0 3.7 reduce_sum.37
  255.8 94.6 %all-to-all-done = bf16[8,160,4096]{2,1,0:T(8,128)(2,1)} async-done(((bf16[8,160,4096]{2,1,0:T(8,128)(2,1)}), bf16[8,160,4096]{2,1,0:T(8,128)(2,1)}, u32[]{:S(2)}, u32[]{:S(2)}) %all-to-all-start) | async-done | bytes 10485792 | tf_op jit(solution)/shard_map/all_to_all | solution.py:71
  350.3 6.8 %fusion.55 = f32[128,4096]{1,0:T(8,128)} fusion(bf16[1280,4096]{1,0:T(8,128)(2,1)} %bitcast.24, s32[128,1280]{1,0:T(8,128)S(1)} %reduce_sum.37), kind=kOutput, calls=%fused_computation.49 | convolution fusion | flops 1342341120 | bytes 13238272 | tf_op jit(solution)/shard_map/tq,qd->td/dot_general | solution.py:86
  357.2 0.0 reduce-scatter.2.cloned.1.call-update
  357.2 0.0 slice-start.2
  357.2 0.0 slice-start.3
  357.2 9.2 %bitcast_convert_fusion.1 = bf16[2,256,4096]{2,1,0:T(8,128)(2,1)} fusion(bf16[8,2,80,256]{3,2,0,1:T(8,128)(2,1)S(1)} %get-tuple-element.6, bf16[8,2,80,4096]{3,2,1,0:T(8,128)(2,1)} %convolution_convert_fusion), kind=kOutput, calls=%fused_computation.8 | convolution fusion | flops 2686451712 | bytes 15335424 | tf_op jit(solution)/shard_map/sxcf,sxcd->xfd/dot_general | solution.py:58
  366.5 9.3 %bitcast_convert_fusion.2 = bf16[2,256,4096]{2,1,0:T(8,128)(2,1)} fusion(bf16[8,2,80,256]{3,2,0,1:T(8,128)(2,1)S(1)} %get-tuple-element.7, bf16[8,2,80,4096]{3,2,1,0:T(8,128)(2,1)} %convolution_convert_fusion), kind=kOutput, calls=%fused_computation.9 | convolution fusion | flops 2686451712 | bytes 15335424 | tf_op jit(solution)/shard_map/sxcf,sxcd->xfd/dot_general | solution.py:55
  375.7 0.0 slice-done.4
  375.8 5.3 %bitcast_convert_fusion = bf16[2,256,4096]{2,1,0:T(8,128)(2,1)} fusion(bf16[8,2,80,4096]{3,2,1,0:T(8,128)(2,1)S(1)} %bitcast.84, f32[8,2,80,256]{3,2,0,1:T(8,128)S(1)} %copy-done.4, f32[8,2,80,256]{3,2,0,1:T(8,128)S(1)} %copy-done.3), kind=kOutput, calls=%fused_computation.7 | convolution fusion | flops 2688417792 | bytes 17301504 | tf_op jit(solution)/shard_map/sxcf,sxcd->xfd/dot_general | solution.py:61
  381.1 19.0 %reduce-scatter.2.cloned.1.call-done = f32[128,1024]{1,0:T(8,128)} async-done(((f32[128,4096]{1,0:T(8,128)}), f32[128,1024]{1,0:T(8,128)}) %reduce-scatter.2.cloned.1.call-update) | async-done | bytes 524304 | tf_op jit(solution)/shard_map/reduce_scatter | solution.py:92
  400.1 1.8 convert_element_type.75
  (21 shorter events, 0.1 us)
Async XLA Ops:
  7.2 62.7 %copy-start.2 = (f32[128,8]{0,1:T(8,128)S(1)}, f32[128,8]{0,1:T(8,128)}, u32[]{:S(2)}) copy-start(f32[128,8]{0,1:T(8,128)} %param.10) | copy-start | bytes 12292
  7.2 51.4 %all-gather.6.cloned.1.call-start = ((), (), s32[]{:S(2)}) async-start(), calls=%async_computation.2 | async-start | bytes 2621440 | tf_op jit(solution)/shard_map/all_gather | solution.py:38
  9.1 140.0 %all-gather.8.cloned.1.call-start = ((), (), s32[]{:S(2)}) async-start(), calls=%async_computation.4 | async-start | bytes 18874368 | tf_op jit(solution)/shard_map/all_gather | solution.py:39
  164.1 18.6 %slice-start = ((s8[8388608]{0:T(1024)(128)(4,1)}), s8[4194304]{0:T(1024)(128)(4,1)S(1)}, s32[]{:S(2)}) async-start(s8[8388608]{0:T(1024)(128)(4,1)} %bitcast.80), calls=%async_computation.5 | async-start | bytes 8388608
  173.3 9.3 %slice-start.1 = ((s8[8388608]{0:T(1024)(128)(4,1)}), s8[4194304]{0:T(1024)(128)(4,1)S(1)}, s32[]{:S(2)}) async-start(s8[8388608]{0:T(1024)(128)(4,1)} %bitcast.80), calls=%async_computation.6 | async-start | bytes 8388608
  188.0 9.4 %copy-start = (bf16[2,256,4096]{2,1,0:T(8,128)(2,1)S(1)}, bf16[2,256,4096]{2,1,0:T(8,128)(2,1)}, u32[]{:S(2)}) copy-start(bf16[2,256,4096]{2,1,0:T(8,128)(2,1)} %param.11) | copy-start | bytes 12582916
  228.5 5.4 %copy-start.1 = (s32[128,8]{0,1:T(8,128)S(1)}, s32[128,8]{0,1:T(8,128)}, u32[]{:S(2)}) copy-start(s32[128,8]{0,1:T(8,128)} %param.9) | copy-start | bytes 12292
  228.5 121.8 %all-to-all-start = ((bf16[8,160,4096]{2,1,0:T(8,128)(2,1)}), bf16[8,160,4096]{2,1,0:T(8,128)(2,1)}, u32[]{:S(2)}, u32[]{:S(2)}) async-start(bf16[8,160,4096]{2,1,0:T(8,128)(2,1)} %bitcast.78), calls=%async_computation | async-start | bytes 20971520 | tf_op jit(solution)/shard_map/all_to_all | solution.py:71
  233.8 166.3 %reduce-scatter.2.cloned.1.call-start = ((), (), s32[]{:S(2)}) async-start(), calls=%async_computation.3 | async-start | bytes 2621440 | tf_op jit(solution)/shard_map/reduce_scatter | solution.py:92
  357.2 18.5 %slice-start.2 = ((s8[10485760]{0:T(1024)(128)(4,1)}), s8[4194304]{0:T(1024)(128)(4,1)S(1)}, s32[]{:S(2)}) async-start(s8[10485760]{0:T(1024)(128)(4,1)} %bitcast.83), calls=%async_computation.7 | async-start | bytes 8388608
  357.2 18.5 %slice-start.3 = ((s8[10485760]{0:T(1024)(128)(4,1)}), s8[4194304]{0:T(1024)(128)(4,1)S(1)}, s32[]{:S(2)}) async-start(s8[10485760]{0:T(1024)(128)(4,1)} %bitcast.83), calls=%async_computation.8 | async-start | bytes 8388608
  366.4 9.3 %slice-start.4 = ((s8[10485760]{0:T(1024)(128)(4,1)}), s8[2097152]{0:T(1024)(128)(4,1)S(1)}, s32[]{:S(2)}) async-start(s8[10485760]{0:T(1024)(128)(4,1)} %bitcast.83), calls=%async_computation.9 | async-start | bytes 4194304
  366.4 9.3 %copy-start.3 = (f32[8,2,80,256]{3,2,0,1:T(8,128)S(1)}, f32[8,2,80,256]{3,2,0,1:T(8,128)}, u32[]{:S(2)}) copy-start(f32[8,2,80,256]{3,2,0,1:T(8,128)} %fusion.35) | copy-start | bytes 3932164
  366.5 9.3 %copy-start.4 = (f32[8,2,80,256]{3,2,0,1:T(8,128)S(1)}, f32[8,2,80,256]{3,2,0,1:T(8,128)}, u32[]{:S(2)}) copy-start(f32[8,2,80,256]{3,2,0,1:T(8,128)} %fusion.30) | copy-start | bytes 3932164
Sparse Core Ops, SparseCore 0:
  10.1 48.3 all-gather.5
  60.4 88.6 all-gather.7
  357.3 42.7 reduce-scatter.1

commit v4 on v3

--- a/solution.py
+++ b/solution.py
@@ -25,8 +25,9 @@
     pair_count = token_count * top_count
     cap_iota = jnp.arange(capacity, dtype=jnp.int32)
 
-    all_ids = lax.all_gather(expert_ids, "expert", axis=0, tiled=False)
-    all_prob = lax.all_gather(route_prob, "expert", axis=0, tiled=False)
+    routing = jnp.stack([expert_ids.astype(jnp.float32), route_prob])
+    routing = lax.all_gather(routing, "expert", axis=1, tiled=False)
+    all_ids, all_prob = routing[0].astype(jnp.int32), routing[1]
     mine = me * local_experts + jnp.arange(local_experts, dtype=jnp.int32)
     named = all_ids.reshape(expert_devices, pair_count)[:, :, None] == mine
     rank = ranks(named)

time: 409 us -> 409 us (level)
  blocking collectives: 18.6 us -> 9.03 us
  waiting for transfers between devices: 230 us -> 238 us
    all_gather x2 -> x1, blocking collectives: 18.6 us -> 9.03 us  [body(): routing = lax.all_gather(routing, 'expert', axis=1, tiled=False)]
    all_gather x1, waiting for transfers between devices: 67.3 us -> 75.3 us  [body(): both = lax.all_gather(both, 'expert', axis=1, tiled=False)]
  transfers between devices with their start and end apart: 4 -> 4, of which waited for: 4 -> 4; matrix products, arithmetic and copies ran while one was open for 12% -> 13% of each run, Pallas kernels for 0% -> 0%
where the time goes in v4:
time: 409 us; the launch traced here: 408 us
  waiting for transfers between devices  238 us (58%)
  matrix products  92.1 us (23%)
  local copies, waits for them, and re-layouts  29.9 us (7%)
  other arithmetic  19.5 us (5%)
  between operations  13.9 us (3%)
  blocking collectives  9.03 us (2%)
  starting transfers between devices  5.41 us (1%)
    all_to_all x1, waiting for transfers between devices, body(): lax.all_to_all(partial_value.reshape(expert_devices, local_experts * capa...  94.6 us
    all_gather x1, waiting for transfers between devices, body(): both = lax.all_gather(both, 'expert', axis=1, tiled=False)  75.3 us
    all_gather x1, waiting for transfers between devices, body(): lax.all_gather(jnp.stack([tokens, grad_out]), 'edata', axis=2, tiled=True)  49.4 us
    reduce_scatter x1, waiting for transfers between devices, body(): lax.psum_scatter(per_token, 'edata', scatter_dimension=1, tiled=True)  19 us
    dot_general x1, matrix products, body(): jnp.einsum('sxcf,xfd->sxcd', up_grad, w_up, preferred_element_type=jnp.fl...  13 us
    slice x1, local copies, waits for them, and re-layouts, body(): all_x, all_dy = (both[0], both[1])  9.49 us
    convert_element_type x1, local copies, waits for them, and re-layouts, body(): partial_value = partial_value.astype(jnp.bfloat16)  9.44 us
    dot_general x1, matrix products, body(): jnp.einsum('sxcd,xfd->sxcf', slot_dy, w_down, preferred_element_type=jnp....  9.36 us
  transfers between devices with their start and end apart: 4, of which 4 were waited for; matrix products, arithmetic and copies ran while one was open for 13% of the time, Pallas kernels for 0%

profile of v4, /device:TPU:0, one launch (start us, length us, event | category | flops | bytes accessed | tf_op | source)
XLA Modules:
  0.0 408.3 jit_solution(9152429621475397026)
XLA Ops:
  7.2 0.0 all-gather.5.cloned.1.call-start
  7.2 1.9 pad_maximum_fusion
  9.1 0.0 all-gather.5.cloned.1.call-update
  9.1 0.0 all-gather.7.cloned.1.call-start
  9.2 49.4 %all-gather.5.cloned.1.call-done = bf16[2,128,4096]{2,1,0:T(8,128)(2,1)} async-done(((bf16[2,128,1024]{2,1,0:T(8,128)(2,1)}), bf16[2,128,4096]{2,1,0:T(8,128)(2,1)}) %all-gather.5.cloned.1.call-update) | async-done | bytes 2097168 | tf_op jit(solution)/shard_map/all_gather | solution.py:39
  58.5 0.0 all-gather.7.cloned.1.call-update
  58.6 0.7 convert_bitcast_fusion
  59.3 0.7 pad_maximum_fusion.1
  59.9 9.0 %all-gather = f32[2,1024,8]{1,2,0:T(8,128)S(1)} all-gather(f32[2,128,8]{1,2,0:T(8,128)S(1)} %pad_maximum_fusion.1), channel_id=2, replica_groups=mesh['edata'=4,'expert'=8] {'expert'}, dimensions={1}, use_global_device_ids=true | all-gather | bytes 73728 | tf_op jit(solution)/shard_map/all_gather | solution.py:29
  69.0 0.1 broadcast_compare_fusion
  69.1 0.2 copy.37
  69.3 0.3 convert_element_type.85
  69.6 0.5 fusion.49
  70.1 0.6 eq.89
  70.7 0.3 copy.38
  71.0 1.3 convert_reduce_fusion
  72.4 1.3 select_reduce_fusion
  73.7 75.3 %all-gather.7.cloned.1.call-done = bf16[2,1024,4096]{2,1,0:T(8,128)(2,1)} async-done(((bf16[2,128,4096]{2,1,0:T(8,128)(2,1)}), bf16[2,1024,4096]{2,1,0:T(8,128)(2,1)}) %all-gather.7.cloned.1.call-update) | async-done | bytes 16777232 | tf_op jit(solution)/shard_map/all_gather | solution.py:40
  149.0 9.5 %fusion.65 = (bf16[1,1024,4096]{2,1,0:T(8,128)(2,1)}, bf16[1,1024,4096]{2,1,0:T(8,128)(2,1)S(1)}) fusion(bf16[2,1024,4096]{2,1,0:T(8,128)(2,1)} %all-gather.7.cloned.1.call-done), kind=kLoop, calls=%fused_computation.65 | loop fusion | bytes 33554432 | tf_op jit(solution)/shard_map/slice | solution.py:41
  158.5 5.5 %convolution_convert_fusion = bf16[8,2,80,4096]{3,2,1,0:T(8,128)(2,1)} fusion(bf16[8,128,4096,1]{2,1,3,0:T(8,128)(2,1)S(1)} %bitcast.84, s32[8,128,2,80]{1,3,2,0:T(8,128)S(1)} %convert_reduce_fusion), kind=kOutput, calls=%fused_computation.11 | convolution fusion | flops 1347584000 | bytes 19529728 | tf_op jit(solution)/shard_map/stxc,std->sxcd/dot_general | solution.py:42
  163.9 9.3 %fusion.35 = f32[8,2,80,256]{3,2,0,1:T(8,128)} fusion(bf16[2,256,4096]{2,1,0:T(8,128)(2,1)} %param.11, bf16[8,2,80,4096]{3,2,1,0:T(8,128)(2,1)} %convolution_convert_fusion), kind=kOutput, calls=%fused_computation.35 | convolution fusion | flops 2684354560 | bytes 15990784 | tf_op jit(solution)/shard_map/sxcd,xfd->sxcf/dot_general | solution.py:48
  173.2 9.3 %fusion.30 = f32[8,2,80,256]{3,2,0,1:T(8,128)} fusion(bf16[2,256,4096]{2,1,0:T(8,128)(2,1)} %param.12, bf16[8,2,80,4096]{3,2,1,0:T(8,128)(2,1)} %convolution_convert_fusion), kind=kOutput, calls=%fused_computation.34 | convolution fusion | flops 2684354560 | bytes 15990784 | tf_op jit(solution)/shard_map/sxcd,xfd->sxcf/dot_general | solution.py:49
  182.5 5.4 %multiply_convert_fusion = bf16[8,2,80,4096]{3,2,1,0:T(8,128)(2,1)} fusion(f32[8,2,80]{2,1,0:T(2,128)S(1)} %select_reduce_fusion, bf16[8,128,4096,1]{2,1,3,0:T(8,128)(2,1)S(1)} %bitcast.87, s32[8,128,2,80]{1,3,2,0:T(8,128)S(1)} %convert_reduce_fusion), kind=kOutput, calls=%fused_computation.1 | convolution fusion | flops 1352826880 | bytes 19534848 | tf_op jit(solution)/shard_map/stxc,std->sxcd/dot_general | solution.py:45
  187.9 9.4 %multiply_convert_fusion.2 = (bf16[8,2,80,256]{3,2,0,1:T(8,128)(2,1)S(1)}, bf16[8,2,80,256]{3,2,0,1:T(8,128)(2,1)S(1)}) fusion(f32[8,2,80,256]{3,2,0,1:T(8,128)} %fusion.35, f32[8,2,80,256]{3,2,0,1:T(8,128)} %fusion.30, bf16[2,256,4096]{2,1,0:T(8,128)(2,1)} %param.13, bf16[8,2,80,4096]{3,2,1,0:T(8,128)(2,1)} %multiply_convert_fusion), kind=kOutput, calls=%fused_computation.38 | convolution fusion | flops 2688614400 | bytes 18612224 | tf_op jit(solution)/shard_map/sxcd,xfd->sxcf/dot_general | solution.py:53
  197.3 8.7 %fusion.20 = f32[2,8,80,4096]{3,2,1,0:T(8,128)} fusion(bf16[8,2,80,256]{3,2,0,1:T(8,128)(2,1)S(1)} %get-tuple-element.7, bf16[2,256,4096]{2,1,0:T(8,128)(2,1)S(1)} %copy-done), kind=kOutput, calls=%fused_computation.24 | convolution fusion | flops 2684354560 | bytes 25821184 | tf_op jit(solution)/shard_map/sxcf,xfd->sxcd/dot_general | solution.py:65
  206.0 13.0 %fusion = bf16[8,2,80,4096]{3,2,0,1:T(8,128)(2,1)} fusion(f32[2,8,80,4096]{3,2,1,0:T(8,128)} %fusion.20, bf16[8,2,80,256]{3,2,0,1:T(8,128)(2,1)S(1)} %get-tuple-element.6, bf16[2,256,4096]{2,1,0:T(8,128)(2,1)} %param.12), kind=kOutput, calls=%fused_computation.2 | convolution fusion | flops 2694840320 | bytes 36306944 | tf_op jit(solution)/shard_map/sxcf,xfd->sxcd/dot_general | solution.py:68
  219.0 9.4 %copy.42 = bf16[8,2,80,4096]{3,2,1,0:T(8,128)(2,1)} copy(bf16[8,2,80,4096]{3,2,0,1:T(8,128)(2,1)} %fusion) | data formatting | bytes 20971520 | tf_op jit(solution)/shard_map/convert_element_type | solution.py:71
  228.4 5.3 %all-to-all-start = ((bf16[8,160,4096]{2,1,0:T(8,128)(2,1)}), bf16[8,160,4096]{2,1,0:T(8,128)(2,1)}, u32[]{:S(2)}, u32[]{:S(2)}) async-start(bf16[8,160,4096]{2,1,0:T(8,128)(2,1)} %bitcast.83), calls=%async_computation | async-start | bytes 20971520 | tf_op jit(solution)/shard_map/all_to_all | solution.py:72
  233.7 0.0 reduce-scatter.2.cloned.1.call-start
  233.8 0.1 copy.34
  233.9 0.1 eq.76
  234.0 0.3 copy.35
  234.3 0.5 fusion.54
  234.8 0.2 iota_compare_fusion.9
  235.0 7.9 %and_convert_fusion = s32[1024,16,80]{2,1,0:T(8,128)} fusion(pred[1024,80]{1,0:T(8,128)(4,1)S(1)} %iota_compare_fusion.9, pred[1024,16]{1,0:T(8,128)(4,1)S(1)} %copy.35), kind=kLoop, calls=%fused_computation.10 | loop fusion | flops 2621440 | bytes 5341184 | tf_op jit(solution)/shard_map/convert_element_type | solution.py:85
  242.8 9.1 %reshape.90 = s32[128,8,1280]{2,1,0:T(8,128)} reshape(s32[1024,16,80]{2,1,0:T(8,128)} %and_convert_fusion) | data formatting | bytes 10485760 | tf_op jit(solution)/shard_map/convert_element_type | solution.py:85
  251.9 3.7 reduce_sum.37
  255.7 94.6 %all-to-all-done = bf16[8,160,4096]{2,1,0:T(8,128)(2,1)} async-done(((bf16[8,160,4096]{2,1,0:T(8,128)(2,1)}), bf16[8,160,4096]{2,1,0:T(8,128)(2,1)}, u32[]{:S(2)}, u32[]{:S(2)}) %all-to-all-start) | async-done | bytes 10485792 | tf_op jit(solution)/shard_map/all_to_all | solution.py:72
  350.2 6.8 %fusion.55 = f32[128,4096]{1,0:T(8,128)} fusion(bf16[1280,4096]{1,0:T(8,128)(2,1)} %bitcast.26, s32[128,1280]{1,0:T(8,128)S(1)} %reduce_sum.37), kind=kOutput, calls=%fused_computation.49 | convolution fusion | flops 1342341120 | bytes 13238272 | tf_op jit(solution)/shard_map/tq,qd->td/dot_general | solution.py:87
  357.1 0.0 reduce-scatter.2.cloned.1.call-update
  357.1 0.0 slice-start.2
  357.1 0.0 slice-start.3
  357.1 9.2 %bitcast_convert_fusion.1 = bf16[2,256,4096]{2,1,0:T(8,128)(2,1)} fusion(bf16[8,2,80,256]{3,2,0,1:T(8,128)(2,1)S(1)} %get-tuple-element.6, bf16[8,2,80,4096]{3,2,1,0:T(8,128)(2,1)} %convolution_convert_fusion), kind=kOutput, calls=%fused_computation.8 | convolution fusion | flops 2686451712 | bytes 15335424 | tf_op jit(solution)/shard_map/sxcf,sxcd->xfd/dot_general | solution.py:59
  366.3 9.3 %bitcast_convert_fusion.2 = bf16[2,256,4096]{2,1,0:T(8,128)(2,1)} fusion(bf16[8,2,80,256]{3,2,0,1:T(8,128)(2,1)S(1)} %get-tuple-element.7, bf16[8,2,80,4096]{3,2,1,0:T(8,128)(2,1)} %convolution_convert_fusion), kind=kOutput, calls=%fused_computation.9 | convolution fusion | flops 2686451712 | bytes 15335424 | tf_op jit(solution)/shard_map/sxcf,sxcd->xfd/dot_general | solution.py:56
  375.6 0.0 slice-done.3
  375.6 5.3 %bitcast_convert_fusion = bf16[2,256,4096]{2,1,0:T(8,128)(2,1)} fusion(bf16[8,2,80,4096]{3,2,1,0:T(8,128)(2,1)S(1)} %bitcast.89, f32[8,2,80,256]{3,2,0,1:T(8,128)S(1)} %copy-done.3, f32[8,2,80,256]{3,2,0,1:T(8,128)S(1)} %copy-done.2), kind=kOutput, calls=%fused_computation.7 | convolution fusion | flops 2688417792 | bytes 17301504 | tf_op jit(solution)/shard_map/sxcf,sxcd->xfd/dot_general | solution.py:62
  381.0 19.0 %reduce-scatter.2.cloned.1.call-done = f32[128,1024]{1,0:T(8,128)} async-done(((f32[128,4096]{1,0:T(8,128)}), f32[128,1024]{1,0:T(8,128)}) %reduce-scatter.2.cloned.1.call-update) | async-done | bytes 524304 | tf_op jit(solution)/shard_map/reduce_scatter | solution.py:93
  400.0 1.8 convert_element_type.96
  (21 shorter events, 0.1 us)
Async XLA Ops:
  7.2 51.4 %all-gather.5.cloned.1.call-start = ((), (), s32[]{:S(2)}) async-start(), calls=%async_computation.2 | async-start | bytes 2621440 | tf_op jit(solution)/shard_map/all_gather | solution.py:39
  9.1 139.9 %all-gather.7.cloned.1.call-start = ((), (), s32[]{:S(2)}) async-start(), calls=%async_computation.4 | async-start | bytes 18874368 | tf_op jit(solution)/shard_map/all_gather | solution.py:40
  163.9 18.6 %slice-start = ((s8[8388608]{0:T(1024)(128)(4,1)}), s8[4194304]{0:T(1024)(128)(4,1)S(1)}, s32[]{:S(2)}) async-start(s8[8388608]{0:T(1024)(128)(4,1)} %bitcast.85), calls=%async_computation.5 | async-start | bytes 8388608
  173.2 9.3 %slice-start.1 = ((s8[8388608]{0:T(1024)(128)(4,1)}), s8[4194304]{0:T(1024)(128)(4,1)S(1)}, s32[]{:S(2)}) async-start(s8[8388608]{0:T(1024)(128)(4,1)} %bitcast.85), calls=%async_computation.6 | async-start | bytes 8388608
  187.9 9.4 %copy-start = (bf16[2,256,4096]{2,1,0:T(8,128)(2,1)S(1)}, bf16[2,256,4096]{2,1,0:T(8,128)(2,1)}, u32[]{:S(2)}) copy-start(bf16[2,256,4096]{2,1,0:T(8,128)(2,1)} %param.11) | copy-start | bytes 12582916
  228.4 5.4 %copy-start.1 = (s32[128,8]{0,1:T(8,128)S(1)}, s32[128,8]{0,1:T(8,128)}, u32[]{:S(2)}) copy-start(s32[128,8]{0,1:T(8,128)} %param.9) | copy-start | bytes 12292
  228.4 121.8 %all-to-all-start = ((bf16[8,160,4096]{2,1,0:T(8,128)(2,1)}), bf16[8,160,4096]{2,1,0:T(8,128)(2,1)}, u32[]{:S(2)}, u32[]{:S(2)}) async-start(bf16[8,160,4096]{2,1,0:T(8,128)(2,1)} %bitcast.83), calls=%async_computation | async-start | bytes 20971520 | tf_op jit(solution)/shard_map/all_to_all | solution.py:72
  233.7 166.3 %reduce-scatter.2.cloned.1.call-start = ((), (), s32[]{:S(2)}) async-start(), calls=%async_computation.3 | async-start | bytes 2621440 | tf_op jit(solution)/shard_map/reduce_scatter | solution.py:93
  357.1 18.5 %slice-start.2 = ((s8[10485760]{0:T(1024)(128)(4,1)}), s8[4194304]{0:T(1024)(128)(4,1)S(1)}, s32[]{:S(2)}) async-start(s8[10485760]{0:T(1024)(128)(4,1)} %bitcast.88), calls=%async_computation.7 | async-start | bytes 8388608
  357.1 18.5 %slice-start.3 = ((s8[10485760]{0:T(1024)(128)(4,1)}), s8[4194304]{0:T(1024)(128)(4,1)S(1)}, s32[]{:S(2)}) async-start(s8[10485760]{0:T(1024)(128)(4,1)} %bitcast.88), calls=%async_computation.8 | async-start | bytes 8388608
  366.3 9.3 %slice-start.4 = ((s8[10485760]{0:T(1024)(128)(4,1)}), s8[2097152]{0:T(1024)(128)(4,1)S(1)}, s32[]{:S(2)}) async-start(s8[10485760]{0:T(1024)(128)(4,1)} %bitcast.88), calls=%async_computation.9 | async-start | bytes 4194304
  366.3 9.3 %copy-start.2 = (f32[8,2,80,256]{3,2,0,1:T(8,128)S(1)}, f32[8,2,80,256]{3,2,0,1:T(8,128)}, u32[]{:S(2)}) copy-start(f32[8,2,80,256]{3,2,0,1:T(8,128)} %fusion.35) | copy-start | bytes 3932164
  366.3 9.3 %copy-start.3 = (f32[8,2,80,256]{3,2,0,1:T(8,128)S(1)}, f32[8,2,80,256]{3,2,0,1:T(8,128)}, u32[]{:S(2)}) copy-start(f32[8,2,80,256]{3,2,0,1:T(8,128)} %fusion.30) | copy-start | bytes 3932164
Sparse Core Ops, SparseCore 0:
  10.1 48.3 all-gather.4
  60.4 88.5 all-gather.6
  357.2 42.7 reduce-scatter.1
